TPU v7x, 32 devices: a whole 2x2x4 slice. The times are simulated.
32 devices in a mesh: ctx: 2 (over core), dp: 16 (over z, y, x).
Axes of the slice: x: 2, y: 2, z: 4, core: 2. Of those that a mesh axis runs over, the one named last changes fastest.
Arguments:
- tokens: bfloat16 [16, 1024, 768], P('dp', 'ctx'), may hold values from -6 to 6
- lengths: int32 [16], P('dp'), may hold values from 256 to 1024, as said below
- qkv_weight: bfloat16 [768, 2304], P('dp'), may hold values from -0.21875 to 0.21875
- query_bias: bfloat16 [768], P('dp'), may hold values from -3 to 3
- value_bias: bfloat16 [768], P('dp'), may hold values from -0.1796875 to 0.1796875
- out_weight: bfloat16 [768, 768], P('dp'), may hold values from -4 to 4
- out_bias: bfloat16 [768], P('dp'), may hold values from -0.59765625 to 0.59765625
- norm1_gain: bfloat16 [768], P('dp'), may hold values from 0.5 to 1.5
- norm1_shift: bfloat16 [768], P('dp'), may hold values from -0.59765625 to 0.59765625
- up_weight: bfloat16 [768, 3072], P('dp'), may hold values from -0.21875 to 0.21875
- up_bias: bfloat16 [3072], P('dp'), may hold values from -3 to 3
- down_weight: bfloat16 [3072, 768], P('dp'), may hold values from -0.109375 to 0.109375
- down_bias: bfloat16 [768], P('dp'), may hold values from -0.59765625 to 0.59765625
- norm2_gain: bfloat16 [768], P('dp'), may hold values from 0.5 to 1.5
- norm2_shift: bfloat16 [768], P('dp'), may hold values from -0.59765625 to 0.59765625
- cotangent: bfloat16 [16, 1024, 768], P('dp', 'ctx'), may hold values from -6 to 6
Outputs:
- output: bfloat16 [16, 1024, 768], P('dp', 'ctx')
- input_grad: float32 [16, 1024, 768], P('dp', 'ctx')
- stream_rms: float32 [3], replicated
- grad_qkv_weight: float32 [768, 2304], P('dp')
- grad_query_bias: float32 [768], P('dp')
- grad_value_bias: float32 [768], P('dp')
- grad_out_weight: float32 [768, 768], P('dp')
- grad_out_bias: float32 [768], P('dp')
- grad_norm1_gain: float32 [768], P('dp')
- grad_norm1_shift: float32 [768], P('dp')
- grad_up_weight: float32 [768, 3072], P('dp')
- grad_up_bias: float32 [3072], P('dp')
- grad_down_weight: float32 [3072, 768], P('dp')
- grad_down_bias: float32 [768], P('dp')
- grad_norm2_gain: float32 [768], P('dp')
- grad_norm2_shift: float32 [768], P('dp')
Inputs may be any that keep to these rules, and one draw needn't show every extreme that they name: The first lengths[b] tokens of sequence b are real and the rest is padding; in every draw some sequence has 1024 valid tokens and some has 256.
All inputs are finite; a program needn't handle non-finite values.
Results may differ from a plain program's by a relative error of at most 0.02.
Values may be sent and summed in bfloat16 or wider, within the bound.
No kernel may reach another device: no remote copies, remote signals or barrier semaphores. Data moves between devices by JAX's collectives and lax.ppermute only.
A program may use at most 128 MiB of HBM per device.

v0:
```python
import math

import jax
import jax.numpy as jnp
from jax import lax
from jax.experimental import pallas as pl
from jax.experimental.pallas import tpu as pltpu
from jax.sharding import PartitionSpec as P

HEADS = 12
LANES = 128
VECTORS = 16
VMEM_BYTES = 24 << 20
FLOPS = 400_000_000
BYTES = 1_200_000

masked_score = -1e30
norm_eps = 1e-05
f32 = jnp.float32
bf16 = jnp.bfloat16


def low_precision(value):
    return lax.reduce_precision(value, exponent_bits=8, mantissa_bits=7)


class Links:
    def __init__(self):
        self.dp = lax.axis_size("dp")
        self.ctx = lax.axis_size("ctx")
        self.bits = self.dp.bit_length() - 1
        assert self.dp == 1 << self.bits and self.bits >= 2 and self.ctx % 2 == 0
        self.core = lax.axis_index("ctx") % 2
        self.me = lax.axis_index("dp")
        self.upper = []
        bit = self.bits - 1
        while bit >= 2:
            size = 2 if (bit - 1) % 2 == 0 else 1
            self.upper.append(tuple(range(bit, bit - size, -1)))
            bit -= size

    def swap(self, value):
        return lax.ppermute(value, "ctx", [(i, i ^ 1) for i in range(self.ctx)])

    def hop(self, value, mask_even, mask_odd):
        pairs = []
        for block in range(self.ctx):
            mask = mask_odd if block % 2 else mask_even
            pairs += [(block * self.dp + i, block * self.dp + (i ^ mask)) for i in range(self.dp)]
        return lax.ppermute(value, ("ctx", "dp"), pairs)

    def places(self, core):
        position = lax.iota(jnp.int32, self.dp)
        quarter = self.dp // 4
        first = (position // quarter) % 2
        second = position // (2 * quarter)
        mask = first * (1 + core) + second * (2 - core)
        for i in range(self.bits - 2):
            mask = mask + ((position >> i) % 2) * (1 << (self.bits - 1 - i))
        return jnp.bitwise_xor(self.me, mask)

    def spots(self, core):
        mask = jnp.bitwise_xor(self.me, lax.iota(jnp.int32, self.dp))
        low, high = mask % 2, (mask // 2) % 2
        first = jnp.where(core == 0, low, high)
        second = jnp.where(core == 0, high, low)
        quarter = self.dp // 4
        spot = first * quarter + second * (2 * quarter)
        for i in range(self.bits - 2):
            spot = spot + ((mask >> (self.bits - 1 - i)) % 2) * (1 << i)
        return spot

    def table(self, *more):
        parts = [self.places(self.core), self.places(1 - self.core)]
        parts += [self.spots(self.core), self.spots(1 - self.core)]
        parts += [jnp.reshape(value, (1,)) for value in (self.core,) + more]
        return jnp.concatenate(parts).astype(jnp.int32)

    def masks(self, bits):
        return [
            sum(((i >> j) & 1) << bit for j, bit in enumerate(bits)) for i in range(1 << len(bits))
        ]

    def cross(self, piece):
        held = [piece]
        for bits in self.upper:
            here = jnp.concatenate(held, axis=0) if len(held) > 1 else held[0]
            held = [here] + [self.hop(here, mask, mask) for mask in self.masks(bits)[1:]]
        return held

    def first(self, held, *waits):
        more = self.hop(held, 1, 2)
        return jnp.concatenate([held, after(more, *waits) if waits else more], axis=0)

    def second(self, held, *waits):
        early = self.swap(held)
        more = self.hop(held, 2, 1)
        if waits:
            early, more = after((early, more), *waits)
        return [held, more], [early, self.swap(more)]


def joined(held, *waits):
    return jnp.concatenate(after(tuple(held), *waits) if waits else held, axis=0)


class Sum:
    def __init__(self, links, kept, direct=False):
        self.links = links
        self.kept = kept
        self.quarter = kept[0].shape[0]
        self.rows = 4 * self.quarter
        self.terms = []
        self.steps = [[(2, 1)], [(1, 2)]]
        for bits in reversed(links.upper):
            if direct:
                self.steps.append([(mask, mask) for mask in links.masks(bits)[1:]])
            else:
                self.steps += [[(1 << bit, 1 << bit)] for bit in reversed(bits)]
        self.ready = None

    def total(self, start, span):
        index = min(2, start // self.quarter)
        first = start - index * self.quarter
        value = self.kept[index]
        if span != value.shape[0]:
            value = lax.slice_in_dim(value, first, first + span, axis=0)
        if not self.terms:
            return value
        value = value.astype(f32)
        for term in self.terms:
            parts = [
                lax.slice_in_dim(part, start, start + span, axis=0).astype(f32) for part in term
            ]
            if len(parts) == 1:
                value = low_precision(value + parts[0])
            else:
                value = low_precision((value + parts[0]) + (parts[1] + parts[2]))
        return value.astype(bf16)

    def prepare(self):
        masks = self.steps[0]
        self.rows //= len(masks) + 1
        self.ready = [self.total((i + 1) * self.rows, self.rows) for i in range(len(masks))]
        return self.ready

    def send(self):
        if self.ready is None:
            self.prepare()
        masks = self.steps.pop(0)
        self.terms.append(
            tuple(self.links.hop(value, *mask) for value, mask in zip(self.ready, masks))
        )
        self.ready = None

    def hold(self, other):
        self.terms[-1] = tuple(after(value, other) for value in self.terms[-1])

    def finish(self):
        while self.steps:
            self.send()
        mine = self.total(0, self.rows)
        step = 2
        while step < self.links.ctx:
            pairs = [(i, i ^ step) for i in range(self.links.ctx)]
            other = lax.ppermute(mine, "ctx", pairs)
            mine = low_precision(mine.astype(f32) + other.astype(f32)).astype(bf16)
            step *= 2
        return mine


def after(value, *others):
    return lax.optimization_barrier((value, others))[0]


def half_columns(links, value):
    span = value.shape[1] // 2
    return lax.dynamic_slice_in_dim(value, links.core * span, span, 1)


def both_halves(links, mine, theirs):
    even = links.core == 0
    return jnp.concatenate(
        [jnp.where(even, mine, theirs), jnp.where(even, theirs, mine)], axis=1
    ).astype(f32)


def dot(left, right):
    return jnp.dot(left, right, preferred_element_type=f32)


def dot_rows(left, right):
    return lax.dot_general(left, right, (((1,), (1,)), ((), ())), preferred_element_type=f32)


def turned(value):
    return jnp.transpose(value)


def aligned(start, size, unit):
    return pl.ds(pl.multiple_of(start, unit), size)


SMEM = pl.BlockSpec(memory_space=pltpu.SMEM)
ANY = pl.BlockSpec(memory_space=pl.ANY)
VMEM = pl.BlockSpec(memory_space=pltpu.VMEM)


def cost(microseconds):
    return pl.CostEstimate(
        flops=int(microseconds * FLOPS), transcendentals=0, bytes_accessed=int(microseconds * BYTES)
    )


def call(body, name, sources, in_specs, outs, scratch=(), time=5):
    return pl.pallas_call(
        body,
        name=name,
        out_shape=outs,
        in_specs=in_specs,
        out_specs=[VMEM] * len(outs),
        scratch_shapes=list(scratch),
        compiler_params=pltpu.CompilerParams(vmem_limit_bytes=VMEM_BYTES),
        cost_estimate=cost(time),
    )(*sources)


def shape(rows, columns, dtype):
    return jax.ShapeDtypeStruct((rows, columns), dtype)


class Piece:
    def __init__(self, dp, rows, columns, first):
        self.dp, self.rows, self.columns, self.first = dp, rows, columns, first

    def fetch(self, scalar, sides, whole, sem):
        core = scalar[4 * self.dp]
        for side, sources in enumerate(sides):
            half = core if side == 0 else 1 - core
            count = self.dp // len(sources)
            for i, source in enumerate(sources):

                def one(position, carry, side=side, source=source, half=half, base=i * count):
                    owner = scalar[side * self.dp + base + position]
                    pltpu.make_async_copy(
                        source.at[
                            aligned(position * self.rows, self.rows, 8),
                            pl.ds(self.first, self.columns),
                        ],
                        whole.at[
                            aligned(owner * self.rows, self.rows, 8),
                            aligned(half * self.columns, self.columns, LANES),
                        ],
                        sem,
                    ).start()
                    return carry

                lax.fori_loop(0, count, one, 0)

    def fetch_side(self, scalar, side, sources, whole, sem):
        count = self.dp // len(sources)
        for i, source in enumerate(sources):

            def one(position, carry, source=source, base=i * count):
                owner = scalar[side * self.dp + base + position]
                pltpu.make_async_copy(
                    source.at[
                        aligned(position * self.rows, self.rows, 8),
                        pl.ds(self.first, self.columns),
                    ],
                    whole.at[aligned(owner * self.rows, self.rows, 8), :],
                    sem,
                ).start()
                return carry

            lax.fori_loop(0, count, one, 0)

    def fetch_rows(self, scalar, part, sides, whole, sem):
        core = scalar[4 * self.dp]
        for side, sources in enumerate(sides):
            half = core if side == 0 else 1 - core
            count = self.dp // len(sources)

            def one(i, carry, side=side, sources=sources, half=half, count=count):
                spot = scalar[(2 + side) * self.dp + part * (self.dp // 2) + i]
                for j, source in enumerate(sources):

                    @pl.when(spot // count == j)
                    def _(source=source, j=j):
                        pltpu.make_async_copy(
                            source.at[
                                aligned((spot - j * count) * self.rows, self.rows, 8),
                                pl.ds(self.first, self.columns),
                            ],
                            whole.at[
                                aligned(i * self.rows, self.rows, 8),
                                aligned(half * self.columns, self.columns, LANES),
                            ],
                            sem,
                        ).start()

                return carry

            lax.fori_loop(0, self.dp // 2, one, 0)

    def ready(self, whole, sem):
        pltpu.make_async_copy(whole, whole, sem).wait()

    def whole(self):
        return pltpu.VMEM((self.dp * self.rows, 2 * self.columns), bf16)


def place(scalar, dp, tile, outs, rows, columns):
    base = 0
    for out in outs:
        count = out.shape[0] // rows

        def one(i, carry, out=out, base=base):
            owner = scalar[base + i]
            out[aligned(i * rows, rows, 8), columns] = tile[aligned(owner * rows, rows, 8), :].astype(
                bf16
            )
            return carry

        lax.fori_loop(0, count, one, 0)
        base += count


def placed(dp, rows, columns):
    return [
        shape(rows * dp // 4, columns, bf16),
        shape(rows * dp // 4, columns, bf16),
        shape(rows * dp // 2, columns, bf16),
    ]


def in_hbm(*dims):
    *dims, dtype = dims
    return pltpu.HBM(tuple(dims), dtype)


def sides(refs):
    return (refs[:2], refs[2:4])


def far(value):
    return pltpu.with_memory_space_constraint(value, pltpu.HBM)


def flat(gathered):
    return [far(value) for value in (*gathered[0], *gathered[1])]


def project(links, table, rows, gathered, qkv_piece, vector_piece, scale, base, folds):
    tokens, width = rows.shape
    shard = width // links.dp

    def body(scalar, rows_ref, *refs):
        q_ref, kv_ref, vec_ref, bias_ref, rows_t_ref, weight, vecs, sems = refs[4:]
        pieces = sides(refs)
        vector_piece.fetch_side(scalar, 0, pieces[0], vecs, sems.at[1])
        qkv_piece.fetch(scalar, pieces, weight, sems.at[0])
        vector_piece.ready(vecs, sems.at[1])
        vectors = turned(vecs[...].astype(f32))[:VECTORS]
        vec_ref[...] = vectors
        bias_ref[...] = jnp.concatenate(
            [
                vectors[base + j : base + j + 1, i * shard : (i + 1) * shard]
                for i in range(links.dp)
                for j in range(folds)
            ],
            axis=1,
        )
        rows_t_ref[...] = turned(rows_ref[...])
        qkv_piece.ready(weight, sems.at[0])
        x = rows_ref[...]
        query = (dot(x, weight[:, :width]) + vectors[0:1]).astype(bf16)
        q_ref[...] = (query.astype(f32) * scale).astype(bf16)
        kv_ref[:, :width] = dot(x, weight[:, width : 2 * width]).astype(bf16)
        kv_ref[:, width:] = (dot(x, weight[:, 2 * width :]) + vectors[1:2]).astype(bf16)

    return call(
        body,
        "qkv",
        [table, rows, *flat(gathered)],
        [SMEM, VMEM] + [ANY] * 4,
        [
            shape(tokens, width, bf16),
            shape(tokens, 2 * width, bf16),
            shape(VECTORS, width, f32),
            shape(1, folds * width, f32),
            shape(width, tokens, bf16),
        ],
        [qkv_piece.whole(), pltpu.VMEM((width, LANES), bf16), pltpu.SemaphoreType.DMA((2,))],
        time=5,
    )


def pair_specs(parts, pairs, base):
    specs = []
    for part in parts:
        rows = part.shape[0]
        specs.append(pl.BlockSpec((rows, LANES), lambda p, s: (0, base + p)))
        specs.append(pl.BlockSpec((rows, LANES), lambda p, s: (0, pairs + base + p)))
    return specs


def first_lanes(shape_, count):
    return (lax.broadcasted_iota(jnp.int32, shape_, 1) < count).astype(f32).astype(bf16)


def head_blocks(query):
    lane = lax.broadcasted_iota(jnp.int32, query.shape, 1)
    zero = jnp.zeros_like(query)
    half = LANES // 2
    return jnp.concatenate(
        [jnp.where(lane < half, query, zero), jnp.where(lane >= half, query, zero)], axis=0
    )


def attend(query, parts, starts, length, base, count):
    tokens, width = query.shape
    pairs = width // LANES
    span = sum(part.shape[0] for part in parts)
    half = LANES // 2
    chunk = min(256, tokens)
    scalars = jnp.concatenate(
        [jnp.reshape(v, (1,)).astype(jnp.int32) for v in [length, *starts]]
    )

    def body(scalar, q_ref, *refs):
        kv_refs = refs[: 2 * len(parts)]
        mixed_t_ref, mixed_ref, p_ref, inverse_ref, bias = refs[2 * len(parts) :]

        @pl.when(pl.program_id(0) == 0)
        def _():
            at = 0
            for i, part in enumerate(parts):
                rows = part.shape[0]
                position = scalar[1 + i] + lax.broadcasted_iota(jnp.int32, (rows, LANES), 0)
                lane = lax.broadcasted_iota(jnp.int32, (rows, LANES), 1)
                hidden = jnp.where(position < scalar[0], 0.0, masked_score)
                bias[at : at + rows, :] = jnp.where(lane == 0, hidden, 0.0).astype(bf16)
                at += rows

        keys = jnp.concatenate([ref[...] for ref in kv_refs[0::2]], axis=0)
        values = jnp.concatenate([ref[...] for ref in kv_refs[1::2]], axis=0)
        keys = jnp.concatenate([keys, bias[...]], axis=1)
        values_t = jnp.concatenate([turned(values), jnp.ones((16, span), bf16)], axis=0)
        queries = head_blocks(q_ref[...])
        queries = jnp.concatenate([queries, first_lanes(queries.shape, 1)], axis=1)
        for at in range(0, 2 * tokens, chunk):
            scores = dot_rows(keys, queries[at : at + chunk])
            peak = jnp.max(scores, axis=0, keepdims=True)
            weights = jnp.exp(scores - peak).astype(bf16)
            p_ref[:, at : at + chunk] = weights
        sums = dot(values_t, p_ref[...])
        inverse = 1.0 / sums[LANES : LANES + 1]
        inverse_ref[...] = inverse
        mixed_t_ref[:half, :] = sums[:half, :tokens] * inverse[:, :tokens]
        mixed_t_ref[half:, :] = sums[half:LANES, tokens:] * inverse[:, tokens:]
        mixed_ref[...] = turned(mixed_t_ref[...]).astype(bf16)

    sources = [query]
    for part in parts:
        sources += [part, part]
    return pl.pallas_call(
        body,
        name="attend",
        cost_estimate=cost(8),
        out_shape=[
            in_hbm(count * LANES, tokens, f32),
            shape(tokens, count * LANES, bf16),
            in_hbm(count, span, 2 * tokens, bf16),
            in_hbm(count, 1, 2 * tokens, f32),
        ],
        grid_spec=pltpu.PrefetchScalarGridSpec(
            num_scalar_prefetch=1,
            grid=(count,),
            in_specs=[pl.BlockSpec((tokens, LANES), lambda p, s: (0, base + p))]
            + pair_specs(parts, pairs, base),
            out_specs=[
                pl.BlockSpec((LANES, tokens), lambda p, s: (p, 0)),
                pl.BlockSpec((tokens, LANES), lambda p, s: (0, p)),
                pl.BlockSpec((None, span, 2 * tokens), lambda p, s: (p, 0, 0)),
                pl.BlockSpec((None, 1, 2 * tokens), lambda p, s: (p, 0, 0)),
            ],
            scratch_shapes=[pltpu.VMEM((span, LANES), bf16)],
        ),
        compiler_params=pltpu.CompilerParams(vmem_limit_bytes=min(56 << 20, VMEM_BYTES * max(1, span // 1024))),
    )(scalars, *sources)


def attend_back(query, parts, grad_mixed, mixed_t, weights, inverse, scale, base, core):
    tokens, width = query.shape
    pairs = width // LANES
    span = sum(part.shape[0] for part in parts)
    half = LANES // 2
    chunk = min(256, tokens)

    def body(_, q_ref, gm_ref, mt_ref, p_ref, inv_ref, *refs):
        kv_refs = refs[: 2 * len(parts)]
        send_ref, keep_ref, ds_ref = refs[2 * len(parts) :]
        keys = jnp.concatenate([ref[...] for ref in kv_refs[0::2]], axis=0)
        values = jnp.concatenate([ref[...] for ref in kv_refs[1::2]], axis=0)
        grads = turned(gm_ref[...].astype(f32))
        inv = inv_ref[...]
        product = grads * mt_ref[...]
        empty = jnp.zeros((half, tokens), bf16)
        even, odd = inv[:, :tokens], inv[:, tokens:]
        delta = jnp.concatenate(
            [
                jnp.sum(product[:half], axis=0, keepdims=True) * even,
                jnp.sum(product[half:], axis=0, keepdims=True) * odd,
            ],
            axis=1,
        )
        top = jnp.concatenate([(grads[:half] * even).astype(bf16), empty], axis=1)
        bottom = jnp.concatenate([empty, (grads[half:] * odd).astype(bf16)], axis=1)
        scaled = jnp.concatenate([top, bottom], axis=0)
        first = (-delta).astype(bf16).astype(f32)
        second = (-delta - first).astype(bf16).astype(f32)
        third = (-delta - first - second).astype(bf16).astype(f32)
        row = lax.broadcasted_iota(jnp.int32, (LANES, 2 * tokens), 0)
        limbs = jnp.where(
            row == 0, first, jnp.where(row == 1, second, jnp.where(row == 2, third, 0.0))
        ).astype(bf16)
        right = jnp.concatenate([scaled, limbs], axis=0)
        left = jnp.concatenate([values, first_lanes(values.shape, 3)], axis=1)
        for at in range(0, 2 * tokens, chunk):
            grad_probs = dot(left, right[:, at : at + chunk])
            ds_ref[:, at : at + chunk] = (
                p_ref[:, at : at + chunk].astype(f32) * grad_probs
            ).astype(bf16)
        grad_scores = ds_ref[...]
        turned_grad = dot(turned(keys), grad_scores)
        grad_query = (
            turned(
                jnp.concatenate([turned_grad[:half, :tokens], turned_grad[half:, tokens:]], axis=0)
            )
            * scale
        ).astype(bf16)
        grad_keys = dot(grad_scores, head_blocks(q_ref[...])).astype(bf16)
        grad_values = dot_rows(p_ref[...], scaled).astype(bf16)
        pieces = [grad_query]
        at = 0
        for part in parts:
            rows = part.shape[0]
            pieces += [grad_keys[at : at + rows], grad_values[at : at + rows]]
            at += rows

        def write(ref, values_, start):
            for value in values_:
                ref[start : start + value.shape[0], :] = value
                start += value.shape[0]

        @pl.when(pl.program_id(0) == 0)
        def _():
            write(send_ref, pieces, 0)

        @pl.when(pl.program_id(0) == 1)
        def _():
            write(keep_ref, pieces[:3], 0)
            write(send_ref, pieces[3:], 5 * tokens)

    local = lambda p, s: (1 - p) * (1 - s[0]) + p * s[0]
    offset = lambda p, s: (0, base + local(p, s))
    sources = [query, grad_mixed, far(mixed_t), far(weights), far(inverse)]
    in_specs = [
        pl.BlockSpec((tokens, LANES), offset),
        pl.BlockSpec((tokens, LANES), offset),
        pl.BlockSpec((LANES, tokens), lambda p, s: (local(p, s), 0)),
        pl.BlockSpec((None, span, 2 * tokens), lambda p, s: (local(p, s), 0, 0)),
        pl.BlockSpec((None, 1, 2 * tokens), lambda p, s: (local(p, s), 0, 0)),
    ]
    for part in parts:
        sources += [part, part]
        rows = part.shape[0]
        in_specs.append(pl.BlockSpec((rows, LANES), offset))
        in_specs.append(pl.BlockSpec((rows, LANES), lambda p, s: (0, pairs + base + local(p, s))))
    kept = tokens + 2 * parts[0].shape[0]
    sent = 7 * tokens if len(parts) == 2 else kept
    return pl.pallas_call(
        body,
        name="attend_back",
        cost_estimate=cost(5),
        out_shape=[shape(sent, LANES, bf16), shape(kept, LANES, bf16)],
        grid_spec=pltpu.PrefetchScalarGridSpec(
            num_scalar_prefetch=1,
            grid=(2,),
            in_specs=in_specs,
            out_specs=[
                pl.BlockSpec((sent, LANES), lambda p, s: (0, 0)),
                pl.BlockSpec((kept, LANES), lambda p, s: (0, 0)),
            ],
            scratch_shapes=[pltpu.VMEM((span, 2 * tokens), bf16)],
        ),
        compiler_params=pltpu.CompilerParams(
            vmem_limit_bytes=min(56 << 20, VMEM_BYTES * max(1, span // 1024))
        ),
    )(jnp.reshape(core, (1,)).astype(jnp.int32), *sources)


def normalize(resid):
    center = resid - jnp.mean(resid, axis=1, keepdims=True)
    inverse = lax.rsqrt(jnp.mean(center * center, axis=1, keepdims=True) + norm_eps)
    return center * inverse, inverse


def norm_back(grads, normal, inverse, gain):
    scaled = grads * gain
    return inverse * (
        scaled
        - jnp.mean(scaled, axis=1, keepdims=True)
        - normal * jnp.mean(scaled * normal, axis=1, keepdims=True)
    )


def column_sums(value):
    return jnp.sum(value, axis=0, keepdims=True)


def by_rows(tokens, body):
    rows = min(tokens, 128)

    def one(i, carry):
        body(aligned(i * rows, rows, 8), i * rows, rows)
        return carry

    lax.fori_loop(0, tokens // rows, one, 0)


def add_row(ref, row, value):
    ref[row : row + 1, :] += value


def spread_total(ref, row):
    lanes = ref[row : row + 1, :]
    ref[row : row + 1, :] = jnp.broadcast_to(jnp.sum(lanes, axis=1, keepdims=True), lanes.shape)


def masked_squares(value, valid):
    return column_sums(jnp.where(valid, value * value, 0.0))


def valid_rows(scalar, at, first, rows):
    position = scalar[at + 1] + first + lax.broadcasted_iota(jnp.int32, (rows, 1), 0)
    return position < scalar[at]


def after_attention(links, table, rows, mixed, vectors, gathered, out_piece):
    tokens, width = rows.shape
    extra = 4 * links.dp + 1
    count = len(mixed)
    part = width // count

    def body(scalar, rows_ref, vec_ref, *refs):
        mixed_refs = refs[:count]
        pieces = sides(refs[count:])
        hidden_ref, low_ref, low_t_ref, mixed_t_ref = refs[count + 4 : count + 8]
        normal_ref, inverse_ref, sums_ref, weight, sem = refs[count + 8 :]
        out_piece.fetch(scalar, pieces, weight, sem.at[0])
        out_piece.ready(weight, sem.at[0])
        for i, ref in enumerate(mixed_refs):
            product = dot(ref[...], weight[i * part : (i + 1) * part, :])
            hidden_ref[...] = product if i == 0 else hidden_ref[...] + product
        sums_ref[...] = jnp.zeros_like(sums_ref)

        def block(at, first, span):
            x = rows_ref[at, :].astype(f32)
            valid = valid_rows(scalar, extra, first, span)
            branch = hidden_ref[at, :] + vec_ref[2:3]
            add_row(sums_ref, 0, masked_squares(x, valid))
            add_row(sums_ref, 1, masked_squares(branch, valid))
            count = jnp.sum(valid.astype(f32), axis=0, keepdims=True)
            add_row(sums_ref, 2, jnp.broadcast_to(count, (1, width)))
            normal, inverse = normalize(x + branch)
            hidden = normal * vec_ref[3:4] + vec_ref[4:5]
            normal_ref[at, :] = normal
            inverse_ref[at, :] = inverse
            hidden_ref[at, :] = hidden
            low_ref[at, :] = hidden.astype(bf16)

        by_rows(tokens, block)
        spread_total(sums_ref, 0)
        spread_total(sums_ref, 1)
        low_t_ref[...] = turned(low_ref[...])
        for i, ref in enumerate(mixed_refs):
            mixed_t_ref[i * part : (i + 1) * part, :] = turned(ref[...])

    return call(
        body,
        "after_attention",
        [table, rows, vectors, *mixed, *flat(gathered)],
        [SMEM] + [VMEM] * (2 + count) + [ANY] * 4,
        [
            shape(tokens, width, f32),
            shape(tokens, width, bf16),
            shape(width, tokens, bf16),
            shape(width, tokens, bf16),
            shape(tokens, width, f32),
            shape(tokens, 1, f32),
            shape(3, width, f32),
        ],
        [out_piece.whole(), pltpu.SemaphoreType.DMA((1,))],
        time=3.5,
    )


def gelu_and_slope(u):
    phi = 0.5 * lax.erf(u * math.sqrt(0.5)) + 0.5
    bell = jnp.exp(-0.5 * (u * u)) * (1.0 / math.sqrt(2.0 * math.pi))
    return u * phi, phi + u * bell


def feed_up(links, table, low, up_bias, gathered, up_piece):
    tokens, width = low.shape
    inner = up_bias.shape[1]

    def body(scalar, low_ref, bias_ref, *refs):
        act_ref, act_t_ref, slope_ref, weight, sem = refs[4:]
        up_piece.fetch(scalar, sides(refs), weight, sem.at[0])
        up_piece.ready(weight, sem.at[0])

        def forward(j, carry):
            at = aligned(j * width, width, LANES)
            value, slope = gelu_and_slope(dot(low_ref[...], weight[:, at]) + bias_ref[:, at])
            value = value.astype(bf16)
            act_ref[:, at] = value
            act_t_ref[at, :] = turned(value)
            slope_ref[:, at] = slope.astype(bf16)
            return carry

        lax.fori_loop(0, inner // width, forward, 0)

    return call(
        body,
        "feed_up",
        [table, low, up_bias, *flat(gathered)],
        [SMEM] + [VMEM] * 2 + [ANY] * 4,
        [
            shape(tokens, inner, bf16),
            shape(inner, tokens, bf16),
            shape(tokens, inner, bf16),
        ],
        [up_piece.whole(), pltpu.SemaphoreType.DMA((1,))],
        time=8,
    )


def share(core, value, at, keep_ref, send_ref):
    span = value.shape[1] // 2
    low, high = value[:, :span], value[:, span:]
    even = core == 0
    keep_ref[at, :] = jnp.where(even, low, high)
    send_ref[at, :] = jnp.where(even, high, low)


def feed_down(links, table, act, hidden, vectors, cotangent, gathered, down_piece):
    tokens, width = hidden.shape
    inner = act.shape[1]
    extra = 4 * links.dp + 1
    dp = links.dp

    def body(scalar, act_ref, hidden_ref, vec_ref, cot_ref, *refs):
        out_ref, resid_ref, grad_ref, keep_ref, send_ref, sums_ref, weight, sem = refs[4:]
        down_piece.fetch(scalar, sides(refs), weight, sem.at[0])
        down_piece.ready(weight, sem.at[0])
        resid_ref[...] = dot(act_ref[...], weight[...])
        sums_ref[...] = jnp.zeros_like(sums_ref)

        def block(at, first, span):
            branch = resid_ref[at, :] + vec_ref[5:6]
            valid = valid_rows(scalar, extra, first, span)
            add_row(sums_ref, 3, masked_squares(branch, valid))
            normal, inverse = normalize(hidden_ref[at, :] + branch)
            out_ref[at, :] = (normal * vec_ref[6:7] + vec_ref[7:8]).astype(bf16)
            grads = cot_ref[at, :].astype(f32)
            add_row(sums_ref, 1, column_sums(grads * normal))
            add_row(sums_ref, 2, column_sums(grads))
            resid = norm_back(grads, normal, inverse, vec_ref[6:7])
            resid_ref[at, :] = resid
            grad_ffn = resid.astype(bf16)
            grad_ref[at, :] = grad_ffn
            add_row(sums_ref, 0, column_sums(grad_ffn.astype(f32)))
            share(scalar[4 * dp], grad_ffn, at, keep_ref, send_ref)

        by_rows(tokens, block)
        spread_total(sums_ref, 3)

    return call(
        body,
        "feed_down",
        [table, act, hidden, vectors, cotangent, *flat(gathered)],
        [SMEM] + [VMEM] * 4 + [ANY] * 4,
        [
            shape(tokens, width, bf16),
            shape(tokens, width, f32),
            shape(tokens, width, bf16),
            shape(tokens, width // 2, bf16),
            shape(tokens, width // 2, bf16),
            shape(4, width, f32),
        ],
        [down_piece.whole(), pltpu.SemaphoreType.DMA((1,))],
        time=6,
    )


def feed_back(links, table, side, slope, so_far, grad_ffn, up, down, pieces):
    tokens, width = so_far.shape
    up_piece, down_piece = pieces
    span = up_piece.columns
    block = width if span % width == 0 else span
    dp = links.dp

    def body(scalar, slope_ref, so_far_ref, grad_ref, um, ul, *refs):
        hidden_ref, out_ref, bias_ref, up_w, down_w, sems = refs[4:]
        core = scalar[4 * dp]
        half = core if side == 0 else 1 - core
        down_piece.fetch_rows(scalar, half, sides(refs), down_w, sems.at[1])
        up_piece.fetch_side(scalar, side, (um, ul), up_w, sems.at[0])
        hidden_ref[...] = so_far_ref[...]
        down_piece.ready(down_w, sems.at[1])
        up_piece.ready(up_w, sems.at[0])

        def backward(j, carry):
            here = aligned(j * block, block, LANES)
            at = aligned(half * span + j * block, block, LANES)
            grads = dot_rows(grad_ref[...], down_w[here, :]) * slope_ref[:, at].astype(f32)
            grads = grads.astype(bf16)
            bias_ref[:, here] = column_sums(grads.astype(f32))
            hidden_ref[...] += dot_rows(grads, up_w[:, here])
            out_ref[:, here] = grads
            return carry

        lax.fori_loop(0, span // block, backward, 0)

    return call(
        body,
        "feed_back",
        [table, slope, so_far, grad_ffn, *map(far, up[side]), *flat(down)],
        [SMEM] + [VMEM] * 3 + [ANY] * 6,
        [shape(tokens, width, f32), shape(tokens, span, bf16), shape(1, span, f32)],
        [
            pltpu.VMEM((width, span), bf16),
            pltpu.VMEM((span, width), bf16),
            pltpu.SemaphoreType.DMA((2,)),
        ],
        time=6,
    )


def before_attention(links, table, grad_hidden, normal, inverse, vectors, gathered, piece):
    tokens, width = normal.shape

    def body(scalar, grad_ref, normal_ref, inverse_ref, vec_ref, *refs):
        resid_ref, gm_ref, keep_ref, send_ref, sums_ref, weight, whole, sem = refs[4:]
        piece.fetch(scalar, sides(refs), weight, sem.at[0])
        sums_ref[...] = jnp.zeros_like(sums_ref)

        def block(at, first, span):
            grads = grad_ref[at, :]
            normal_ = normal_ref[at, :]
            add_row(sums_ref, 1, column_sums(grads * normal_))
            add_row(sums_ref, 2, column_sums(grads))
            resid = norm_back(grads, normal_, inverse_ref[at, :], vec_ref[3:4])
            resid_ref[at, :] = resid
            grad_attn = resid.astype(bf16)
            whole[at, :] = grad_attn
            add_row(sums_ref, 0, column_sums(grad_attn.astype(f32)))
            share(scalar[4 * links.dp], grad_attn, at, keep_ref, send_ref)

        by_rows(tokens, block)
        piece.ready(weight, sem.at[0])
        gm_ref[...] = dot_rows(whole[...], weight[...]).astype(bf16)

    return call(
        body,
        "before_attention",
        [table, grad_hidden, normal, inverse, vectors, *flat(gathered)],
        [SMEM] + [VMEM] * 4 + [ANY] * 4,
        [
            shape(tokens, width, f32),
            shape(tokens, width, bf16),
            shape(tokens, width // 2, bf16),
            shape(tokens, width // 2, bf16),
            shape(3, width, f32),
        ],
        [piece.whole(), pltpu.VMEM((tokens, width), bf16), pltpu.SemaphoreType.DMA((1,))],
        time=0.01,
    )


def weight_gradient(name, links, table, left, right, rows):
    outer, tokens = left[0].shape
    columns = right[0].shape[1]
    block = min(outer, 768)
    wide = min(columns, 512)

    def body(scalar, lm, lt, rm, rt, *refs):
        tile = refs[-1]

        def one(j, carry):
            at = aligned(j // (columns // wide) * block, block, 8)
            to = aligned(j % (columns // wide) * wide, wide, LANES)
            tile[at, to] = dot(lm[at, :], rm[:, to]) + dot(lt[at, :], rt[:, to])
            return carry

        lax.fori_loop(0, outer // block * (columns // wide), one, 0)
        place(scalar, links.dp, tile, refs[:3], rows, slice(None))

    return call(
        body,
        name,
        [table, *left, *right],
        [SMEM] + [VMEM] * 4,
        placed(links.dp, rows, columns),
        [pltpu.VMEM((outer, columns), f32)],
    )


class Shares:
    def __init__(self, refs, tokens):
        self.sent, self.kept, self.came = refs
        self.tokens = tokens

    def rows(self, ref, i):
        return ref[i * self.tokens : (i + 1) * self.tokens, :]

    def add(self, one, other):
        return (one.astype(f32) + other.astype(f32)).astype(bf16)

    def own(self):
        return [self.rows(self.kept, 0)] + [
            self.add(self.rows(self.kept, i), self.rows(self.came, 2 + i)) for i in (1, 2)
        ]

    def others(self):
        return [self.rows(self.came, 0)] + [
            self.add(self.rows(self.sent, 4 + i), self.rows(self.came, i)) for i in (1, 2)
        ]

    def partners(self):
        return [self.rows(self.sent, 0)] + [
            self.add(self.rows(self.sent, i), self.rows(self.came, 4 + i)) for i in (1, 2)
        ]


def attention_gradient(name, links, table, rows_t, groups, rows, out=None, vectors=None, folds=0, sums=()):
    width, tokens = rows_t[0].shape
    dp = links.dp
    wide = 3 * LANES
    half = width // 2
    total = wide * len(groups) + (half if out else 0) + (LANES if vectors is not None else 0)
    given = [value for group in groups for value in group]
    more = list(out or []) + ([*vectors, *sums] if vectors is not None else [])

    def body(scalar, xm, xt, *refs):
        group_refs = refs[: len(given)]
        more_refs = list(refs[len(given) : len(given) + len(more)])
        outs = refs[len(given) + len(more) :]
        sum_ref, tile = outs[3], outs[4]
        for g in range(len(groups)):
            shares = Shares(group_refs[3 * g : 3 * g + 3], tokens)
            mine = jnp.concatenate(shares.own(), axis=1)
            theirs = jnp.concatenate(shares.others(), axis=1)
            tile[:, g * wide : (g + 1) * wide] = dot(xm[...], mine) + dot(xt[...], theirs)
            sums_ = column_sums(mine.astype(f32)) + column_sums(theirs.astype(f32))
            sum_ref[g : g + 1, :] = sums_
        at = wide * len(groups)
        if out:
            mm, mt, gm, gt = more_refs[:4]
            tile[:, at : at + half] = dot(mm[...], gm[...]) + dot(mt[...], gt[...])
            at += half
        if vectors is not None:
            sums3, sums2, kept, sent, sums1, *sum_refs = more_refs
            even = scalar[4 * dp] == 0
            bias = jnp.concatenate(
                [
                    jnp.where(even, kept[...], sent[...]),
                    jnp.where(even, sent[...], kept[...]),
                ],
                axis=1,
            )
            biases = [
                jnp.concatenate(
                    [
                        bias[:, (i * folds + j) * rows : (i * folds + j + 1) * rows]
                        for i in range(dp)
                    ],
                    axis=1,
                )
                for j in range(folds)
            ]
            head = jnp.concatenate(
                [jnp.zeros((2, width), f32), sums3[...], sums2[0:3]]
                + biases
                + [sums1[...], sums2[3:4]],
                axis=0,
            )
            every = [ref[i : i + 1, :] for ref in sum_refs for i in range(ref.shape[0])]
            every += [sum_ref[g : g + 1, :] for g in range(len(groups))]
            lane = lax.broadcasted_iota(jnp.int32, (1, width), 1)
            owned = (lane // LANES) % 2 == scalar[4 * dp]
            lines = []
            for j in (0, 2):
                parts = [s[:, j * LANES : (j + 1) * LANES] for s in every for _ in range(2)]
                lines.append(jnp.where(owned, jnp.concatenate(parts, axis=1), 0.0))
            row = lax.broadcasted_iota(jnp.int32, (LANES, width), 0)
            padded = jnp.concatenate(
                [head, jnp.zeros((LANES - head.shape[0], width), f32)], axis=0
            )
            padded = jnp.where(row == 0, lines[0], jnp.where(row == 1, lines[1], padded))
            tile[:, at : at + LANES] = turned(padded)
        place(scalar, dp, tile, outs[:3], rows, slice(None))

    return call(
        body,
        name,
        [table, *rows_t, *given, *more],
        [SMEM] + [VMEM] * (2 + len(given) + len(more)),
        placed(dp, rows, total) + [shape(len(groups), wide, f32)],
        [pltpu.VMEM((width, total), f32)],
    )


def input_gradient(links, table, groups, resid, gathered, qkv_piece):
    tokens, width = resid.shape
    given = [value for group in groups for value in group]

    def body(scalar, resid_ref, *refs):
        group_refs = refs[: len(given)]
        out_ref, weight, grads, sem = refs[len(given) + 4 :]
        qkv_piece.fetch(scalar, sides(refs[len(given) :]), weight, sem.at[0])
        core = scalar[4 * links.dp]
        for g in range(len(groups)):
            shares = Shares(group_refs[3 * g : 3 * g + 3], tokens)
            for owner, values in ((core, shares.own()), (1 - core, shares.partners())):
                for j, value in enumerate(values):
                    at = j * width + (2 * g + owner) * LANES
                    grads[:, aligned(at, LANES, LANES)] = value
        qkv_piece.ready(weight, sem.at[0])
        out_ref[...] = resid_ref[...] + dot_rows(grads[...], weight[...])

    return call(
        body,
        "input_gradient",
        [table, resid, *given, *flat(gathered)],
        [SMEM] + [VMEM] * (1 + len(given)) + [ANY] * 4,
        [shape(tokens, width, f32)],
        [qkv_piece.whole(), pltpu.VMEM((tokens, 3 * width), bf16), pltpu.SemaphoreType.DMA((1,))],
        time=20,
    )[0]


def closing(links, table, early, late, folds, width):
    rows = early[0].shape[0]
    wide = 3 * LANES
    half = width // 2
    base = 8

    def body(scalar, em, et, lm, lt, *outs):
        qkv_ref, out_ref, *vec_refs, up_ref, rms_ref = outs

        def write(core):
            for owner, early_ref, late_ref in ((core, em, lm), (1 - core, et, lt)):
                groups = [(early_ref, 0), (early_ref, wide), (late_ref, 0)]
                for g, (ref, first) in enumerate(groups):
                    for j in range(3):
                        at = j * width + (2 * g + owner) * LANES
                        qkv_ref[:, at : at + LANES] = ref[
                            :, first + j * LANES : first + (j + 1) * LANES
                        ].astype(f32)
                out_ref[:, owner * half : (owner + 1) * half] = early_ref[
                    :, 2 * wide : 2 * wide + half
                ].astype(f32)

        for core in range(2):
            pl.when(scalar[4 * links.dp] == core)(lambda core=core: write(core))
        last = slice(wide, wide + LANES)
        vectors = turned(lm[:, last].astype(f32) + lt[:, last].astype(f32))
        for i, ref in enumerate(vec_refs):
            ref[...] = vectors[i : i + 1]
        for i in range(folds):
            up_ref[:, i * rows : (i + 1) * rows] = vectors[base + i : base + i + 1]
        at = base + folds
        count = vectors[at + 2 : at + 3] * width
        for i, line in enumerate((at, at + 1, at + 3)):
            value = jnp.sqrt(vectors[line : line + 1] / count + 1e-06)
            rms_ref[:, i : i + 1] = value[:, 0:1]

    return call(
        body,
        "closing",
        [table, *early, *late],
        [SMEM] + [VMEM] * 4,
        [shape(rows, 3 * width, f32), shape(rows, width, f32)]
        + [shape(1, rows, f32)] * base
        + [shape(1, folds * rows, f32), shape(1, 3, f32)],
    )


def settle(links, reduction):
    mine = reduction.finish()
    return mine, links.swap(mine)


def shards(
    tokens,
    lengths,
    qkv_weight,
    query_bias,
    value_bias,
    out_weight,
    out_bias,
    norm1_gain,
    norm1_shift,
    up_weight,
    up_bias,
    down_weight,
    down_bias,
    norm2_gain,
    norm2_shift,
    cotangent,
):
    seq_dev, ctx_tok, width = tokens.shape
    assert seq_dev == 1 and width // HEADS == LANES // 2
    scale = (width // HEADS) ** (-0.5)
    links = Links()
    dp = links.dp
    rows = tokens.reshape(ctx_tok, width)
    cot = cotangent.reshape(ctx_tok, width)
    block = lax.axis_index("ctx")
    start = block * ctx_tok
    table = links.table(lengths[0], start)

    shard = qkv_weight.shape[0]
    inner = down_weight.shape[0] * dp
    folds = down_weight.shape[0] // shard
    half = [w.shape[1] // 2 for w in (qkv_weight, out_weight, up_weight, down_weight)]
    qkv_piece = Piece(dp, shard, half[0], 0)
    vector_piece = Piece(dp, shard, LANES, half[0])
    up_piece = Piece(dp, shard, half[2], 0)
    out_piece = Piece(dp, shard, half[1], half[2])
    down_piece = Piece(dp, down_weight.shape[0], half[3], 0)
    ffn_pieces = (up_piece, down_piece)

    columns = [query_bias, value_bias, out_bias, norm1_gain, norm1_shift]
    columns += [down_bias, norm2_gain, norm2_shift]
    base = len(columns)
    columns += [up_bias[i * shard : (i + 1) * shard] for i in range(folds)]
    packed = jnp.stack(columns, axis=1)
    packed = jnp.pad(packed, ((0, 0), (0, LANES - packed.shape[1])))
    qkv_sent = jnp.concatenate([half_columns(links, qkv_weight), packed], axis=1)
    up_sent = jnp.concatenate(
        [half_columns(links, up_weight), half_columns(links, out_weight)], axis=1
    )
    down_sent = half_columns(links, down_weight)

    qkv_held = joined(links.cross(qkv_sent))
    up_held = links.cross(after(up_sent, qkv_held))
    down_sent = after(down_sent, up_held)
    qkv_held = links.first(qkv_held)
    qkv = links.second(after(qkv_held, up_held[1]), *up_held)
    up_held = after(joined(up_held), qkv[0][1])
    query, kv, vectors, up_bias_row, rows_t = project(
        links, table, after(rows, up_held), qkv, qkv_piece, vector_piece, scale, base, folds
    )
    down_held = links.cross(after(down_sent, up_held))
    up_held = links.first(up_held, query)
    kv = after(kv, up_held)
    rows_t = [rows_t, links.swap(rows_t)]
    if links.ctx == 2:
        parts = [kv, links.swap(kv)]
        starts = [start, (1 - block) * ctx_tok]
    else:
        parts = [lax.all_gather(kv, "ctx", axis=0, tiled=True)]
        starts = [jnp.int32(0)]
    groups = 3
    count = width // LANES // groups
    forward = []
    waits = [(), (), ()]
    for i in range(groups):
        given = after(query, *waits[i], *(forward[-1][1:2] if forward else ()))
        forward.append(attend(given, parts, starts, lengths[0], i * count, count))
        if i == 0:
            down_held = joined(down_held, forward[0][1])
            waits[1] = (down_held,)
    up = links.second(up_held, forward[1][1])
    down_held = links.first(after(down_held, forward[1][1]), forward[2][1])
    mixed = [f[1] for f in forward]
    hidden, low, low_t, mixed_t, normal, deviation, sums1 = after_attention(
        links, table, after(rows, down_held), mixed, vectors, up, out_piece
    )
    low_t = [low_t, links.swap(low_t)]
    mixed_t = [mixed_t, links.swap(mixed_t)]
    act, act_t, slope = feed_up(links, table, low, up_bias_row, up, up_piece)
    down = links.second(after(down_held, forward[2][1]), act)
    act_t = [act_t, links.swap(after(act_t, down[1][1]))]
    output, resid2, grad_ffn, ffn_keep, ffn_send, sums2 = feed_down(
        links, table, act, hidden, vectors, cot, down, down_piece
    )
    ffn_came = links.swap(ffn_send)
    grad_hidden, upper_send, bias_sent = feed_back(
        links, table, 1, slope, resid2, grad_ffn, up, down, ffn_pieces
    )
    upper_came = links.swap(upper_send)
    down_sum = Sum(
        links,
        weight_gradient(
            "down_gradient",
            links,
            table,
            [after(act_t[0], grad_hidden), act_t[1]],
            [ffn_keep, ffn_came],
            down_piece.rows,
        ),
    )
    given = after(grad_hidden, down_sum.prepare())
    down_sum.send()
    grad_hidden, upper_keep, bias_kept = feed_back(
        links, table, 0, slope, given, grad_ffn, up, down, ffn_pieces
    )
    up_sum = Sum(
        links,
        weight_gradient(
            "up_gradient", links, table, low_t, [upper_keep, upper_came], up_piece.rows
        ),
    )
    given = after(grad_hidden, up_sum.prepare())
    up_sum.send()
    resid1, grad_mixed, attn_keep, attn_send, sums3 = before_attention(
        links, table, given, normal, deviation, vectors, up, out_piece
    )
    out_parts = [*mixed_t, attn_keep, links.swap(attn_send)]

    def back_through(i, given):
        turned_mixed, _, weights, inverse = forward[i]
        sent, kept = attend_back(
            given,
            parts,
            grad_mixed,
            turned_mixed,
            weights,
            inverse,
            scale,
            i * count,
            links.core,
        )
        if links.ctx == 2:
            return [sent, kept, links.swap(sent)]
        whole = []
        for value in (sent, kept):
            keys, values = jnp.split(value[ctx_tok:], 2, axis=0)
            both = lax.psum_scatter(
                jnp.concatenate([keys, values], axis=1), "ctx", scatter_dimension=0, tiled=True
            )
            whole.append([value[:ctx_tok], both[:, :LANES], both[:, LANES:]])
        blank = jnp.zeros((4 * ctx_tok, LANES), bf16)
        sent = jnp.concatenate(whole[0] + [blank], axis=0)
        return [sent, jnp.concatenate(whole[1], axis=0), links.swap(sent)]

    down_sum.hold(grad_mixed)
    given = after(query, down_sum.prepare(), grad_mixed)
    down_sum.send()
    back = [back_through(0, given)]
    back.append(back_through(1, after(query, back[0][1])))
    down_sum.hold(back[1][1])
    up_sum.hold(back[1][1])
    given = after(rows_t[0], down_sum.prepare(), up_sum.prepare())
    down_sum.send()
    up_sum.send()
    *early, early_sums = attention_gradient(
        "early_gradient", links, table, [given, rows_t[1]], back[:2], shard, out=out_parts
    )
    early_sum = Sum(links, early)
    down_sum.hold(early[2])
    up_sum.hold(early[2])
    given = after(query, early_sum.prepare(), down_sum.prepare(), up_sum.prepare())
    early_sum.send()
    down_sum.send()
    up_sum.send()
    back.append(back_through(2, given))
    up_sum.hold(back[2][1])
    early_sum.hold(back[2][1])
    down_sum.hold(back[2][1])
    up_sum.hold(back[2][1])
    down_mine = down_sum.finish()
    given = after(rows_t[0], early_sum.prepare(), up_sum.prepare(), down_mine)
    early_sum.send()
    up_sum.send()
    *late, _ = attention_gradient(
        "late_gradient",
        links,
        table,
        [given, rows_t[1]],
        back[2:],
        shard,
        vectors=[sums3, sums2, bias_kept, bias_sent, sums1],
        folds=folds,
        sums=[early_sums],
    )
    late_sum = Sum(links, late, direct=True)
    early_sum.hold(late[2])
    up_sum.hold(late[2])
    up_mine = up_sum.finish()
    given = after(resid1, late_sum.prepare(), early_sum.prepare(), up_mine)
    late_sum.send()
    early_sum.send()
    input_grad = input_gradient(links, table, back, given, qkv, qkv_piece)
    late_sum.hold(input_grad)
    early_sum.hold(input_grad)
    down_grad = both_halves(links, down_mine, links.swap(down_mine))
    up_grad = both_halves(links, up_mine, links.swap(up_mine))
    early = settle(links, early_sum)
    late = settle(links, late_sum)
    qkv_grad, out_grad, *sums, up_bias_grad, stream_rms = closing(
        links, table, early, late, folds, width
    )
    sums = [value.reshape(shard) for value in sums]
    return (
        output.reshape(seq_dev, ctx_tok, width),
        input_grad.reshape(seq_dev, ctx_tok, width),
        stream_rms.reshape(3),
        qkv_grad,
        sums[0],
        sums[1],
        out_grad,
        sums[2],
        sums[3],
        sums[4],
        up_grad,
        up_bias_grad.reshape(-1),
        down_grad,
        sums[5],
        sums[6],
        sums[7],
    )


def solution(mesh):
    in_specs = (
        P("dp", "ctx", None),
        P("dp"),
        P("dp", None),
        P("dp"),
        P("dp"),
        P("dp", None),
        P("dp"),
        P("dp"),
        P("dp"),
        P("dp", None),
        P("dp"),
        P("dp", None),
        P("dp"),
        P("dp"),
        P("dp"),
        P("dp", "ctx", None),
    )
    out_specs = (
        P("dp", "ctx", None),
        P("dp", "ctx", None),
        P(),
        P("dp", None),
        P("dp"),
        P("dp"),
        P("dp", None),
        P("dp"),
        P("dp"),
        P("dp"),
        P("dp", None),
        P("dp"),
        P("dp", None),
        P("dp"),
        P("dp"),
        P("dp"),
    )
    return jax.shard_map(shards, mesh=mesh, in_specs=in_specs, out_specs=out_specs, check_vma=False)
```

profile of v0, /device:TPU:0, one launch (start us, length us, event | category | flops | bytes accessed | tf_op | source)
XLA Modules:
  0.0 234.5 jit_solution(15837719855071087434)
XLA Ops:
  3.4 5.1 %collective-permute-start.2 = (bf16[48,1280]{1,0:T(8,128)(2,1)S(1)}, bf16[48,1280]{1,0:T(8,128)(2,1)S(1)}, u32[]{:S(2)}, u32[]{:S(2)}) collective-permute-start(bf16[48,1280]{1,0:T(8,128)(2,1)S(1)} %get-tuple-element.268), channel_id=1, source_target_pairs={{0,12},{1,13},{2,14},{3,15},{4,8},{5,9},{6,10},{7,11},{8,4},{9,5},... | collective-permute-start | bytes 368648 | tf_op jit(solution)/shard_map/ppermute | solution.py:50
  21.5 6.4 %collective-permute-done.6 = bf16[192,1280]{1,0:T(8,128)(2,1)S(1)} collective-permute-done((bf16[192,1280]{1,0:T(8,128)(2,1)S(1)}, bf16[192,1280]{1,0:T(8,128)(2,1)S(1)}, u32[]{:S(2)}, u32[]{:S(2)}) %collective-permute-start.6) | collective-permute-done | bytes 491552 | tf_op jit(solution)/shard_map/ppermute | solution.py:50
  33.0 6.2 %collective-permute-done.4 = bf16[48,1920]{1,0:T(8,128)(2,1)S(1)} collective-permute-done((bf16[48,1920]{1,0:T(8,128)(2,1)S(1)}, bf16[48,1920]{1,0:T(8,128)(2,1)S(1)}, u32[]{:S(2)}, u32[]{:S(2)}) %collective-permute-start.4) | collective-permute-done | bytes 184352 | tf_op jit(solution)/shard_map/ppermute | solution.py:50
  48.4 4.9 %qkv.1 = (bf16[512,768]{1,0:T(8,128)(2,1)S(1)}, bf16[512,1536]{1,0:T(8,128)(2,1)S(1)}, f32[16,768]{1,0:T(8,128)S(1)}, f32[1,3072]{1,0:T(1,128)S(1)}, bf16[768,512]{1,0:T(8,128)(2,1)S(1)}) custom-call(s32[67]{0:T(128)S(1)} %concatenate.39.scalar, bf16[512,768]{1,0:T(8,128)(2,1)S(1)} %bitcast.34, bf16[384,1280]{1,0:T(8,128)(2,1)} %copy-done.16, ...), custom_call_target="tpu_custom_call" | custom-call | flops 2000000000 | bytes 6000000 | tf_op jit(solution)/shard_map/qkv/pallas_call | solution.py:216
  67.1 6.2 %attend.3 = (f32[256,512]{1,0:T(8,128)}, bf16[512,256]{1,0:T(8,128)(2,1)S(1)}, bf16[2,1024,1024]{2,1,0:T(8,128)(2,1)}, f32[2,1,1024]{2,1,0:T(1,128)}) custom-call(s32[3]{0:T(128)S(1)} %pad_add_fusion.scalar, bf16[512,768]{1,0:T(8,128)(2,1)S(1)} %copy-done.3, bf16[512,1536]{1,0:T(8,128)(2,1)S(1)} %get-tuple-element.149.refs_0_.refs_1_, ...), custom_call_target="tpu_custom_call" | custom-call | flops 3200000000 | bytes 9600000 | tf_op jit(solution)/shard_map/attend/pallas_call | solution.py:467
  73.4 6.2 %attend.4 = (f32[256,512]{1,0:T(8,128)}, bf16[512,256]{1,0:T(8,128)(2,1)S(1)}, bf16[2,1024,1024]{2,1,0:T(8,128)(2,1)}, f32[2,1,1024]{2,1,0:T(1,128)}) custom-call(s32[3]{0:T(128)S(1)} %pad_add_fusion.scalar, bf16[512,768]{1,0:T(8,128)(2,1)S(1)} %copy-done.3, bf16[512,1536]{1,0:T(8,128)(2,1)S(1)} %get-tuple-element.149.refs_0_.refs_1_, ...), custom_call_target="tpu_custom_call" | custom-call | flops 3200000000 | bytes 9600000 | tf_op jit(solution)/shard_map/attend/pallas_call | solution.py:467
  81.3 6.2 %attend.5 = (f32[256,512]{1,0:T(8,128)}, bf16[512,256]{1,0:T(8,128)(2,1)S(1)}, bf16[2,1024,1024]{2,1,0:T(8,128)(2,1)}, f32[2,1,1024]{2,1,0:T(1,128)}) custom-call(s32[3]{0:T(128)S(1)} %pad_add_fusion.scalar, bf16[512,768]{1,0:T(8,128)(2,1)S(1)} %copy-done.3, bf16[512,1536]{1,0:T(8,128)(2,1)S(1)} %get-tuple-element.149.refs_0_.refs_1_, ...), custom_call_target="tpu_custom_call" | custom-call | flops 3200000000 | bytes 9600000 | tf_op jit(solution)/shard_map/attend/pallas_call | solution.py:467
  91.6 4.4 %after_attention.1 = (f32[512,768]{1,0:T(8,128)S(1)}, bf16[512,768]{1,0:T(8,128)(2,1)S(1)}, bf16[768,512]{1,0:T(8,128)(2,1)S(1)}, bf16[768,512]{1,0:T(8,128)(2,1...) custom-call(s32[67]{0:T(128)S(1)} %concatenate.39.scalar, ...), custom_call_target="tpu_custom_call" | custom-call | flops 1400000000 | bytes 4200000 | tf_op jit(solution)/shard_map/after_attention/pallas_call | solution.py:216
  96.1 8.5 %feed_up.1 = (bf16[512,3072]{1,0:T(8,128)(2,1)S(1)}, bf16[3072,512]{1,0:T(8,128)(2,1)S(1)}, bf16[512,3072]{1,0:T(8,128)(2,1)S(1)}) custom-call(s32[67]{0:T(128)S(1)} %concatenate.39.scalar, bf16[512,768]{1,0:T(8,128)(2,1)S(1)} %get-tuple-element.165.low_ref, f32[1,3072]{1,0:T(1,128)S(1)} %get-tuple-element.166.bias_ref, ...), custom_call_target="tpu_custom_call" | custom-call | flops 3200000000 | bytes 9600000 | tf_op jit(solution)/shard_map/feed_up/pallas_call | solution.py:216
  110.0 8.1 %feed_down.1 = (bf16[512,768]{1,0:T(8,128)(2,1)}, f32[512,768]{1,0:T(8,128)S(1)}, bf16[512,768]{1,0:T(8,128)(2,1)S(1)}, bf16[512,384]{1,0:T(8,128)(2,1)S(1)}, bf...) custom-call(s32[67]{0:T(128)S(1)} %concatenate.39.scalar, bf16[512,3072]{1,0:T(8,128)(2,1)S(1)} %get-tuple-element.167.act_ref, ...), custom_call_target="tpu_custom_call" | custom-call | flops 2400000000 | bytes 7200000 | tf_op jit(solution)/shard_map/feed_down/pallas_call | solution.py:216
  118.1 6.2 %feed_back.2 = (f32[512,768]{1,0:T(8,128)S(1)}, bf16[512,1536]{1,0:T(8,128)(2,1)S(1)}, f32[1,1536]{1,0:T(1,128)S(1)}) custom-call(s32[67]{0:T(128)S(1)} %concatenate.39.scalar, bf16[512,3072]{1,0:T(8,128)(2,1)S(1)} %get-tuple-element.173.slope_ref, f32[512,768]{1,0:T(8,128)S(1)} %get-tuple-element.174.so_far_ref, ...), custom_call_target="tpu_custom_call" | custom-call | flops 2400000000 | bytes 7200000 | tf_op jit(solution)/shard_map/feed_back/pallas_call | solution.py:216
  128.4 4.8 %down_gradient.1 = (bf16[768,384]{1,0:T(8,128)(2,1)S(1)}, bf16[768,384]{1,0:T(8,128)(2,1)S(1)}, bf16[1536,384]{1,0:T(8,128)(2,1)S(1)}) custom-call(s32[67]{0:T(128)S(1)} %concatenate.39.scalar, bf16[3072,512]{1,0:T(8,128)(2,1)S(1)} %get-tuple-element.179.lm, bf16[3072,512]{1,0:T(8,128)(2,1)S(1)} %collective-permute-done.22.lt, ...), custom_call_target="tpu_custom_call" | custom-call | flops 2000000000 | bytes 6000000 | tf_op jit(solution)/shard_map/down_gradient/pallas_call | solution.py:216
  133.9 6.2 %feed_back.3 = (f32[512,768]{1,0:T(8,128)S(1)}, bf16[512,1536]{1,0:T(8,128)(2,1)S(1)}, f32[1,1536]{1,0:T(1,128)S(1)}) custom-call(s32[67]{0:T(128)S(1)} %concatenate.39.scalar, bf16[512,3072]{1,0:T(8,128)(2,1)S(1)} %get-tuple-element.173.slope_ref, f32[512,768]{1,0:T(8,128)S(1)} %get-tuple-element.183.so_far_ref, ...), custom_call_target="tpu_custom_call" | custom-call | flops 2400000000 | bytes 7200000 | tf_op jit(solution)/shard_map/feed_back/pallas_call | solution.py:216
  140.1 3.8 %up_gradient.1 = (bf16[192,1536]{1,0:T(8,128)(2,1)S(1)}, bf16[192,1536]{1,0:T(8,128)(2,1)S(1)}, bf16[384,1536]{1,0:T(8,128)(2,1)S(1)}) custom-call(s32[67]{0:T(128)S(1)} %concatenate.39.scalar, bf16[768,512]{1,0:T(8,128)(2,1)S(1)} %get-tuple-element.185.lm, bf16[768,512]{1,0:T(8,128)(2,1)S(1)} %collective-permute-done.24.lt, ...), custom_call_target="tpu_custom_call" | custom-call | flops 2000000000 | bytes 6000000 | tf_op jit(solution)/shard_map/up_gradient/pallas_call | solution.py:216
  151.2 6.3 %attend_back.3 = (bf16[3584,128]{1,0:T(8,128)(2,1)S(1)}, bf16[1536,128]{1,0:T(8,128)(2,1)S(1)}) custom-call(s32[1]{0:T(128)} %bitcast._, bf16[512,768]{1,0:T(8,128)(2,1)S(1)} %copy-done.4, bf16[512,768]{1,0:T(8,128)(2,1)S(1)} %get-tuple-element.195.gm_ref, f32[256,512]{1,0:T(8,128)} %get-tuple-element.199.mt_ref, ...), custom_call_target="tpu_custom_call" | custom-call | flops 2000000000 | bytes 6000000 | tf_op jit(solution)/shard_map/attend_back/pallas_call | solution.py:583
  158.0 6.4 %attend_back.4 = (bf16[3584,128]{1,0:T(8,128)(2,1)S(1)}, bf16[1536,128]{1,0:T(8,128)(2,1)S(1)}) custom-call(s32[1]{0:T(128)} %bitcast._, bf16[512,768]{1,0:T(8,128)(2,1)S(1)} %copy-done.4, bf16[512,768]{1,0:T(8,128)(2,1)S(1)} %get-tuple-element.195.gm_ref, f32[256,512]{1,0:T(8,128)} %get-tuple-element.204.mt_ref, ...), custom_call_target="tpu_custom_call" | custom-call | flops 2000000000 | bytes 6000000 | tf_op jit(solution)/shard_map/attend_back/pallas_call | solution.py:583
  164.6 3.8 %collective-permute-done.28 = bf16[384,1536]{1,0:T(8,128)(2,1)S(1)} collective-permute-done((bf16[384,1536]{1,0:T(8,128)(2,1)S(1)}, bf16[384,1536]{1,0:T(8,128)(2,1)S(1)}, u32[]{:S(2)}, u32[]{:S(2)}) %collective-permute-start.28) | collective-permute-done | bytes 1179680 | tf_op jit(solution)/shard_map/ppermute | solution.py:50
  170.8 3.4 %collective-permute-start.35 = (bf16[384,384]{1,0:T(8,128)(2,1)S(1)}, bf16[384,384]{1,0:T(8,128)(2,1)S(1)}, u32[]{:S(2)}, u32[]{:S(2)}) collective-permute-start(bf16[384,384]{1,0:T(8,128)(2,1)S(1)} %reduce-precision_convert_fusion.4), channel_id=1, source_target_pairs={{0,4},{1,5},{2,6},{3,7},{4,0},{5,1},{6,2},{7,3},{8,12},{9,13},{10,... | collective-permute-start | bytes 884744 | tf_op jit(solution)/shard_map/ppermute | solution.py:50
  174.2 3.5 %early_gradient.1 = (bf16[192,1152]{1,0:T(8,128)(2,1)S(1)}, bf16[192,1152]{1,0:T(8,128)(2,1)S(1)}, bf16[384,1152]{1,0:T(8,128)(2,1)S(1)}, f32[2,384]{1,0:T(2,128)S(1)}) custom-call(s32[67]{0:T(128)S(1)} %concatenate.39.scalar, bf16[768,512]{1,0:T(8,128)(2,1)S(1)} %copy-done.7, bf16[768,512]{1,0:T(8,128)(2,1)S(1)} %collective-permute-done.29.xt, ...), custom_call_target="tpu_custom_call" | custom-call | flops 2000000000 | bytes 6000000 | tf_op jit(solution)/shard_map/early_gradient/pallas_call | solution.py:216
  178.2 3.4 %collective-permute-done.35 = bf16[384,384]{1,0:T(8,128)(2,1)S(1)} collective-permute-done((bf16[384,384]{1,0:T(8,128)(2,1)S(1)}, bf16[384,384]{1,0:T(8,128)(2,1)S(1)}, u32[]{:S(2)}, u32[]{:S(2)}) %collective-permute-start.35) | collective-permute-done | bytes 294944 | tf_op jit(solution)/shard_map/ppermute | solution.py:50
  184.7 6.2 %attend_back.5 = (bf16[3584,128]{1,0:T(8,128)(2,1)S(1)}, bf16[1536,128]{1,0:T(8,128)(2,1)S(1)}) custom-call(s32[1]{0:T(128)} %bitcast._, bf16[512,768]{1,0:T(8,128)(2,1)S(1)} %copy-done.4, bf16[512,768]{1,0:T(8,128)(2,1)S(1)} %get-tuple-element.195.gm_ref, f32[256,512]{1,0:T(8,128)} %get-tuple-element.223.mt_ref, ...), custom_call_target="tpu_custom_call" | custom-call | flops 2000000000 | bytes 6000000 | tf_op jit(solution)/shard_map/attend_back/pallas_call | solution.py:583
  204.1 4.6 %collective-permute-done.40 = bf16[192,1152]{1,0:T(8,128)(2,1)S(1)} collective-permute-done((bf16[192,1152]{1,0:T(8,128)(2,1)S(1)}, bf16[192,1152]{1,0:T(8,128)(2,1)S(1)}, u32[]{:S(2)}, u32[]{:S(2)}) %collective-permute-start.40) | collective-permute-done | bytes 442400 | tf_op jit(solution)/shard_map/ppermute | solution.py:50
  208.8 5.8 %input_gradient.1 = f32[512,768]{1,0:T(8,128)} custom-call(s32[67]{0:T(128)S(1)} %concatenate.39.scalar, f32[512,768]{1,0:T(8,128)S(1)} %get-tuple-element.243.resid_ref, bf16[3584,128]{1,0:T(8,128)(2,1)S(1)} %get-tuple-element.212.refs_0_, bf16[1536,128]{1,0:T(8,128)(2,1)S(1)} %get-tuple-element.202.refs_1_, ...), custom_call_target="tpu_custom_call" | custom-call | flops 8000000000 | bytes 24000000 | tf_op jit(solution)/shard_map/input_gradient/pallas_call | solution.py:216
  216.3 4.1 %collective-permute-done.46 = bf16[192,512]{1,0:T(8,128)(2,1)S(1)} collective-permute-done((bf16[192,512]{1,0:T(8,128)(2,1)S(1)}, bf16[192,512]{1,0:T(8,128)(2,1)S(1)}, u32[]{:S(2)}, u32[]{:S(2)}) %collective-permute-start.46) | collective-permute-done | bytes 196640 | tf_op jit(solution)/shard_map/ppermute | solution.py:50
  (184 shorter events, 101.6 us)
Async XLA Ops:
  30.8 11.3 %collective-permute-start.7 = (bf16[384,1280]{1,0:T(8,128)(2,1)S(1)}, bf16[384,1280]{1,0:T(8,128)(2,1)S(1)}, u32[]{:S(2)}, u32[]{:S(2)}) collective-permute-start(bf16[384,1280]{1,0:T(8,128)(2,1)S(1)} %constant_dynamic-update-slice_fusion.refs_0_.refs_9_), channel_id=1, source_target_pairs={{0,16},{16,0},{1,17},{17,1},{2,18},{18,2},{3,19},{19,3},{4,20},{20... | collective-permute-start | bytes 2949128 | tf_op jit(solution)/shard_map/ppermute | solution.py:43
  30.8 14.2 %collective-permute-start.8 = (bf16[384,1280]{1,0:T(8,128)(2,1)S(1)}, bf16[384,1280]{1,0:T(8,128)(2,1)}, u32[]{:S(2)}, u32[]{:S(2)}) collective-permute-start(bf16[384,1280]{1,0:T(8,128)(2,1)S(1)} %constant_dynamic-update-slice_fusion.refs_0_.refs_9_), channel_id=1, source_target_pairs={{0,2},{1,3},{2,0},{3,1},{4,6},{5,7},{6,4},{7,5},{8,10},{9,11},{10,... | collective-permute-start | bytes 2949128 | tf_op jit(solution)/shard_map/ppermute | solution.py:50
  45.1 11.6 %collective-permute-start.13 = (bf16[192,1920]{1,0:T(8,128)(2,1)S(1)}, bf16[192,1920]{1,0:T(8,128)(2,1)}, u32[]{:S(2)}, u32[]{:S(2)}) collective-permute-start(bf16[192,1920]{1,0:T(8,128)(2,1)S(1)} %pad_maximum_fusion), channel_id=1, source_target_pairs={{0,1},{1,0},{2,3},{3,2},{4,5},{5,4},{6,7},{7,6},{8,9},{9,8},{10,11... | collective-permute-start | bytes 2211848 | tf_op jit(solution)/shard_map/ppermute | solution.py:50
  58.8 20.8 %collective-permute-start.16 = (bf16[384,1920]{1,0:T(8,128)(2,1)}, bf16[384,1920]{1,0:T(8,128)(2,1)}, u32[]{:S(2)}, u32[]{:S(2)}) collective-permute-start(bf16[384,1920]{1,0:T(8,128)(2,1)} %constant_dynamic-update-slice_fusion.5.refs_3_.refs_0_.um), channel_id=1, source_target_pairs={{0,16},{16,0},{1,17},{17,1},{2,18},{18,2},{3,19},{19,3},{4,20},{20... | collective-permute-start | bytes 4423688 | tf_op jit(solution)/shard_map/ppermute | solution.py:43
  59.3 20.3 %collective-permute-start.17 = (bf16[384,1920]{1,0:T(8,128)(2,1)}, bf16[384,1920]{1,0:T(8,128)(2,1)}, u32[]{:S(2)}, u32[]{:S(2)}) collective-permute-start(bf16[384,1920]{1,0:T(8,128)(2,1)} %constant_dynamic-update-slice_fusion.5.refs_3_.refs_0_.um), channel_id=1, source_target_pairs={{0,2},{1,3},{2,0},{3,1},{4,6},{5,7},{6,4},{7,5},{8,10},{9,11},{10,... | collective-permute-start | bytes 4423688 | tf_op jit(solution)/shard_map/ppermute | solution.py:50
  59.9 13.4 %collective-permute-start.9 = (bf16[192,384]{1,0:T(8,128)(2,1)S(1)}, bf16[192,384]{1,0:T(8,128)(2,1)S(1)}, u32[]{:S(2)}, u32[]{:S(2)}) collective-permute-start(bf16[192,384]{1,0:T(8,128)(2,1)S(1)} %constant_dynamic-slice_fusion.3), channel_id=1, source_target_pairs={{0,8},{1,9},{2,10},{3,11},{4,12},{5,13},{6,14},{7,15},{8,0},{9,1},... | collective-permute-start | bytes 442376 | tf_op jit(solution)/shard_map/ppermute | solution.py:50
  60.9 12.3 %collective-permute-start.10 = (bf16[192,384]{1,0:T(8,128)(2,1)S(1)}, bf16[192,384]{1,0:T(8,128)(2,1)S(1)}, u32[]{:S(2)}, u32[]{:S(2)}) collective-permute-start(bf16[192,384]{1,0:T(8,128)(2,1)S(1)} %constant_dynamic-slice_fusion.3), channel_id=1, source_target_pairs={{0,4},{1,5},{2,6},{3,7},{4,0},{5,1},{6,2},{7,3},{8,12},{9,13},{10,... | collective-permute-start | bytes 442376 | tf_op jit(solution)/shard_map/ppermute | solution.py:50
  79.6 10.9 %collective-permute-start.18 = (bf16[384,1920]{1,0:T(8,128)(2,1)}, bf16[384,1920]{1,0:T(8,128)(2,1)S(1)}, u32[]{:S(2)}, u32[]{:S(2)}) collective-permute-start(bf16[384,1920]{1,0:T(8,128)(2,1)} %collective-permute-done.17.refs_4_.refs_1_.ul), channel_id=1, source_target_pairs={{0,16},{16,0},{1,17},{17,1},{2,18},{18,2},{3,19},{19,3},{4,20},{20... | collective-permute-start | bytes 4423688 | tf_op jit(solution)/shard_map/ppermute | solution.py:43
  89.7 14.9 %collective-permute-start.19 = (bf16[1536,384]{1,0:T(8,128)(2,1)S(1)}, bf16[1536,384]{1,0:T(8,128)(2,1)S(1)}, u32[]{:S(2)}, u32[]{:S(2)}) collective-permute-start(bf16[1536,384]{1,0:T(8,128)(2,1)S(1)} %constant_dynamic-update-slice_fusion.11.refs_0_), channel_id=1, source_target_pairs={{0,16},{16,0},{1,17},{17,1},{2,18},{18,2},{3,19},{19,3},{4,20},{20... | collective-permute-start | bytes 3538952 | tf_op jit(solution)/shard_map/ppermute | solution.py:43
  89.8 16.3 %collective-permute-start.20 = (bf16[1536,384]{1,0:T(8,128)(2,1)S(1)}, bf16[1536,384]{1,0:T(8,128)(2,1)S(1)}, u32[]{:S(2)}, u32[]{:S(2)}) collective-permute-start(bf16[1536,384]{1,0:T(8,128)(2,1)S(1)} %constant_dynamic-update-slice_fusion.11.refs_0_), channel_id=1, source_target_pairs={{0,2},{1,3},{2,0},{3,1},{4,6},{5,7},{6,4},{7,5},{8,10},{9,11},{10,... | collective-permute-start | bytes 3538952 | tf_op jit(solution)/shard_map/ppermute | solution.py:50
  108.9 19.4 %collective-permute-start.22 = (bf16[3072,512]{1,0:T(8,128)(2,1)S(1)}, bf16[3072,512]{1,0:T(8,128)(2,1)S(1)}, u32[]{:S(2)}, u32[]{:S(2)}) collective-permute-start(bf16[3072,512]{1,0:T(8,128)(2,1)S(1)} %get-tuple-element.179.lm), channel_id=1, source_target_pairs={{0,16},{16,0},{1,17},{17,1},{2,18},{18,2},{3,19},{19,3},{4,20},{20... | collective-permute-start | bytes 9437192 | tf_op jit(solution)/shard_map/ppermute | solution.py:43
  124.3 15.8 %collective-permute-start.25 = (bf16[512,1536]{1,0:T(8,128)(2,1)S(1)}, bf16[512,1536]{1,0:T(8,128)(2,1)S(1)}, u32[]{:S(2)}, u32[]{:S(2)}) collective-permute-start(bf16[512,1536]{1,0:T(8,128)(2,1)S(1)} %get-tuple-element.187), channel_id=1, source_target_pairs={{0,16},{16,0},{1,17},{17,1},{2,18},{18,2},{3,19},{19,3},{4,20},{20... | collective-permute-start | bytes 4718600 | tf_op jit(solution)/shard_map/ppermute | solution.py:43
  124.9 15.2 %collective-permute-start.24 = (bf16[768,512]{1,0:T(8,128)(2,1)S(1)}, bf16[768,512]{1,0:T(8,128)(2,1)S(1)}, u32[]{:S(2)}, u32[]{:S(2)}) collective-permute-start(bf16[768,512]{1,0:T(8,128)(2,1)S(1)} %get-tuple-element.185.lm), channel_id=1, source_target_pairs={{0,16},{16,0},{1,17},{17,1},{2,18},{18,2},{3,19},{19,3},{4,20},{20... | collective-permute-start | bytes 2359304 | tf_op jit(solution)/shard_map/ppermute | solution.py:43
  133.2 16.3 %collective-permute-start.26 = (bf16[1536,384]{1,0:T(8,128)(2,1)S(1)}, bf16[1536,384]{1,0:T(8,128)(2,1)S(1)}, u32[]{:S(2)}, u32[]{:S(2)}) collective-permute-start(bf16[1536,384]{1,0:T(8,128)(2,1)S(1)} %get-tuple-element.182), channel_id=1, source_target_pairs={{0,2},{1,3},{2,0},{3,1},{4,6},{5,7},{6,4},{7,5},{8,10},{9,11},{10,... | collective-permute-start | bytes 3538952 | tf_op jit(solution)/shard_map/ppermute | solution.py:50
  143.9 24.5 %collective-permute-start.28 = (bf16[384,1536]{1,0:T(8,128)(2,1)S(1)}, bf16[384,1536]{1,0:T(8,128)(2,1)S(1)}, u32[]{:S(2)}, u32[]{:S(2)}) collective-permute-start(bf16[384,1536]{1,0:T(8,128)(2,1)S(1)} %get-tuple-element.188), channel_id=1, source_target_pairs={{0,2},{1,3},{2,0},{3,1},{4,6},{5,7},{6,4},{7,5},{8,10},{9,11},{10,... | collective-permute-start | bytes 3538952 | tf_op jit(solution)/shard_map/ppermute | solution.py:50
  149.6 18.8 %collective-permute-start.27 = (bf16[768,384]{1,0:T(8,128)(2,1)S(1)}, bf16[768,384]{1,0:T(8,128)(2,1)S(1)}, u32[]{:S(2)}, u32[]{:S(2)}) collective-permute-start(bf16[768,384]{1,0:T(8,128)(2,1)S(1)} %reduce-precision_convert_fusion.1), channel_id=1, source_target_pairs={{0,1},{1,0},{2,3},{3,2},{4,5},{5,4},{6,7},{7,6},{8,9},{9,8},{10,11... | collective-permute-start | bytes 1769480 | tf_op jit(solution)/shard_map/ppermute | solution.py:50
  151.2 17.9 %collective-permute-start.29 = (bf16[768,512]{1,0:T(8,128)(2,1)S(1)}, bf16[768,512]{1,0:T(8,128)(2,1)S(1)}, u32[]{:S(2)}, u32[]{:S(2)}) collective-permute-start(bf16[768,512]{1,0:T(8,128)(2,1)S(1)} %copy-done.7), channel_id=1, source_target_pairs={{0,16},{16,0},{1,17},{17,1},{2,18},{18,2},{3,19},{19,3},{4,20},{20... | collective-permute-start | bytes 2359304 | tf_op jit(solution)/shard_map/ppermute | solution.py:43
  157.5 16.7 %collective-permute-start.30 = (bf16[3584,128]{1,0:T(8,128)(2,1)S(1)}, bf16[3584,128]{1,0:T(8,128)(2,1)S(1)}, u32[]{:S(2)}, u32[]{:S(2)}) collective-permute-start(bf16[3584,128]{1,0:T(8,128)(2,1)S(1)} %get-tuple-element.212.refs_0_), channel_id=1, source_target_pairs={{0,16},{16,0},{1,17},{17,1},{2,18},{18,2},{3,19},{19,3},{4,20},{20... | collective-permute-start | bytes 2752520 | tf_op jit(solution)/shard_map/ppermute | solution.py:43
  169.1 12.5 %collective-permute-start.36 = (bf16[192,1536]{1,0:T(8,128)(2,1)S(1)}, bf16[192,1536]{1,0:T(8,128)(2,1)S(1)}, u32[]{:S(2)}, u32[]{:S(2)}) collective-permute-start(bf16[192,1536]{1,0:T(8,128)(2,1)S(1)} %reduce-precision_convert_fusion), channel_id=1, source_target_pairs={{0,1},{1,0},{2,3},{3,2},{4,5},{5,4},{6,7},{7,6},{8,9},{9,8},{10,11... | collective-permute-start | bytes 1769480 | tf_op jit(solution)/shard_map/ppermute | solution.py:50
  177.7 19.4 %collective-permute-start.34 = (bf16[384,1152]{1,0:T(8,128)(2,1)S(1)}, bf16[384,1152]{1,0:T(8,128)(2,1)S(1)}, u32[]{:S(2)}, u32[]{:S(2)}) collective-permute-start(bf16[384,1152]{1,0:T(8,128)(2,1)S(1)} %get-tuple-element.218), channel_id=1, source_target_pairs={{0,2},{1,3},{2,0},{3,1},{4,6},{5,7},{6,4},{7,5},{8,10},{9,11},{10,... | collective-permute-start | bytes 2654216 | tf_op jit(solution)/shard_map/ppermute | solution.py:50
  181.8 11.8 %collective-permute-start.37 = (bf16[96,1536]{1,0:T(8,128)(2,1)S(1)}, bf16[96,1536]{1,0:T(8,128)(2,1)S(1)}, u32[]{:S(2)}, u32[]{:S(2)}) collective-permute-start(bf16[96,1536]{1,0:T(8,128)(2,1)S(1)} %reduce-precision_convert_fusion.3), channel_id=1, source_target_pairs={{0,4},{1,5},{2,6},{3,7},{4,0},{5,1},{6,2},{7,3},{8,12},{9,13},{10,... | collective-permute-start | bytes 884744 | tf_op jit(solution)/shard_map/ppermute | solution.py:50
  197.3 11.4 %collective-permute-start.40 = (bf16[192,1152]{1,0:T(8,128)(2,1)S(1)}, bf16[192,1152]{1,0:T(8,128)(2,1)S(1)}, u32[]{:S(2)}, u32[]{:S(2)}) collective-permute-start(bf16[192,1152]{1,0:T(8,128)(2,1)S(1)} %reduce-precision_convert_fusion.2), channel_id=1, source_target_pairs={{0,1},{1,0},{2,3},{3,2},{4,5},{5,4},{6,7},{7,6},{8,9},{9,8},{10,11... | collective-permute-start | bytes 1327112 | tf_op jit(solution)/shard_map/ppermute | solution.py:50
  200.8 13.9 %collective-permute-start.45 = (bf16[384,512]{1,0:T(8,128)(2,1)S(1)}, bf16[384,512]{1,0:T(8,128)(2,1)S(1)}, u32[]{:S(2)}, u32[]{:S(2)}) collective-permute-start(bf16[384,512]{1,0:T(8,128)(2,1)S(1)} %get-tuple-element.239), channel_id=1, source_target_pairs={{0,2},{1,3},{2,0},{3,1},{4,6},{5,7},{6,4},{7,5},{8,10},{9,11},{10,... | collective-permute-start | bytes 1179656 | tf_op jit(solution)/shard_map/ppermute | solution.py:50
  204.0 11.7 %collective-permute-start.51 = (bf16[48,1536]{1,0:T(8,128)(2,1)S(1)}, bf16[48,1536]{1,0:T(8,128)(2,1)S(1)}, u32[]{:S(2)}, u32[]{:S(2)}) collective-permute-start(bf16[48,1536]{1,0:T(8,128)(2,1)S(1)} %reduce-precision_convert_fusion.7), channel_id=1, source_target_pairs={{0,16},{16,0},{1,17},{17,1},{2,18},{18,2},{3,19},{19,3},{4,20},{20... | collective-permute-start | bytes 442376 | tf_op jit(solution)/shard_map/ppermute | solution.py:43
  (47 other events, 304.9 us)
where the time goes:
time: 235 us
  Pallas kernels  101 us (43%)
  waiting for transfers between devices  72.8 us (31%)
  starting transfers between devices  44.6 us (19%)
  local copies, waits for them, and re-layouts  11 us (5%)
  other arithmetic  3.61 us (2%)
    ppermute x32, waiting for transfers between devices, hop(): return lax.ppermute(value, ('ctx', 'dp'), pairs)  64 us
    pallas_call x13, Pallas kernels, call(): pl.pallas_call(body, name=name, out_shape=outs, in_specs=in_specs, out_sp...  63 us
    ppermute x32, starting transfers between devices, hop(): return lax.ppermute(value, ('ctx', 'dp'), pairs)  41.6 us
    pallas_call x3, Pallas kernels, attend_back(): pl.pallas_call(body, name='attend_back', cost_estimate=cost(5), out_shape...  18.9 us
    pallas_call x3, Pallas kernels, attend(): pl.pallas_call(body, name='attend', cost_estimate=cost(8), out_shape=[in_...  18.6 us
    ppermute x21, waiting for transfers between devices, swap(): return lax.ppermute(value, 'ctx', [(i, i ^ 1) for i in range(self.ctx)])  8.79 us
    unnamed x44, local copies, waits for them, and re-layouts  5.16 us
  transfers between devices with their start and end apart: 53, of which 26 were waited for; matrix products, arithmetic and copies ran while one was open for 2% of the time, Pallas kernels for 42%

commit v1 on v0

--- a/solution.py
+++ b/solution.py
@@ -86,6 +86,18 @@
         for bits in self.upper:
             here = jnp.concatenate(held, axis=0) if len(held) > 1 else held[0]
             held = [here] + [self.hop(here, mask, mask) for mask in self.masks(bits)[1:]]
+        return held
+
+    def cross_slowly(self, piece, ready):
+        held = piece
+        masks = [1 << bit for bits in self.upper for bit in bits]
+        for i, mask in enumerate(masks):
+            more = self.hop(held, mask, mask)
+            if i < len(masks) - 1:
+                more = ready(more)
+            held = [held, more]
+            if i < len(masks) - 1:
+                held = jnp.concatenate(held, axis=0)
         return held
 
     def first(self, held, *waits):
@@ -389,7 +401,7 @@
             shape(tokens, 2 * width, bf16),
             shape(VECTORS, width, f32),
             shape(1, folds * width, f32),
-            shape(width, tokens, bf16),
+            in_hbm(width, tokens, bf16),
         ],
         [qkv_piece.whole(), pltpu.VMEM((width, LANES), bf16), pltpu.SemaphoreType.DMA((2,))],
         time=5,
@@ -846,7 +858,7 @@
             pltpu.VMEM((span, width), bf16),
             pltpu.SemaphoreType.DMA((2,)),
         ],
-        time=6,
+        time=0.01,
     )
 
 
@@ -1166,9 +1178,15 @@
     query, kv, vectors, up_bias_row, rows_t = project(
         links, table, after(rows, up_held), qkv, qkv_piece, vector_piece, scale, base, folds
     )
-    down_held = links.cross(after(down_sent, up_held))
+    early_steps = []
+
+    def ready(more):
+        early_steps.append(more)
+        return after(more, query)
+
+    down_held = links.cross_slowly(after(down_sent, up_held), ready)
     up_held = links.first(up_held, query)
-    kv = after(kv, up_held)
+    kv = after(kv, up_held, *early_steps)
     rows_t = [rows_t, links.swap(rows_t)]
     if links.ctx == 2:
         parts = [kv, links.swap(kv)]
@@ -1201,25 +1219,20 @@
         links, table, act, hidden, vectors, cot, down, down_piece
     )
     ffn_came = links.swap(ffn_send)
-    grad_hidden, upper_send, bias_sent = feed_back(
-        links, table, 1, slope, resid2, grad_ffn, up, down, ffn_pieces
-    )
-    upper_came = links.swap(upper_send)
     down_sum = Sum(
         links,
         weight_gradient(
-            "down_gradient",
-            links,
-            table,
-            [after(act_t[0], grad_hidden), act_t[1]],
-            [ffn_keep, ffn_came],
-            down_piece.rows,
+            "down_gradient", links, table, act_t, [ffn_keep, ffn_came], down_piece.rows
         ),
     )
-    given = after(grad_hidden, down_sum.prepare())
+    given = after(resid2, down_sum.prepare())
     down_sum.send()
+    grad_hidden, upper_send, bias_sent = feed_back(
+        links, table, 1, slope, given, grad_ffn, up, down, ffn_pieces
+    )
+    upper_came = links.swap(upper_send)
     grad_hidden, upper_keep, bias_kept = feed_back(
-        links, table, 0, slope, given, grad_ffn, up, down, ffn_pieces
+        links, table, 0, slope, grad_hidden, grad_ffn, up, down, ffn_pieces
     )
     up_sum = Sum(
         links,
@@ -1227,8 +1240,10 @@
             "up_gradient", links, table, low_t, [upper_keep, upper_came], up_piece.rows
         ),
     )
-    given = after(grad_hidden, up_sum.prepare())
+    down_sum.hold(grad_hidden)
+    given = after(grad_hidden, up_sum.prepare(), down_sum.prepare())
     up_sum.send()
+    down_sum.send()
     resid1, grad_mixed, attn_keep, attn_send, sums3 = before_attention(
         links, table, given, normal, deviation, vectors, up, out_piece
     )
@@ -1260,9 +1275,7 @@
         sent = jnp.concatenate(whole[0] + [blank], axis=0)
         return [sent, jnp.concatenate(whole[1], axis=0), links.swap(sent)]
 
-    down_sum.hold(grad_mixed)
-    given = after(query, down_sum.prepare(), grad_mixed)
-    down_sum.send()
+    given = after(query, grad_mixed)
     back = [back_through(0, given)]
     back.append(back_through(1, after(query, back[0][1])))
     down_sum.hold(back[1][1])
@@ -1285,8 +1298,7 @@
     early_sum.hold(back[2][1])
     down_sum.hold(back[2][1])
     up_sum.hold(back[2][1])
-    down_mine = down_sum.finish()
-    given = after(rows_t[0], early_sum.prepare(), up_sum.prepare(), down_mine)
+    given = after(rows_t[0], early_sum.prepare(), up_sum.prepare())
     early_sum.send()
     up_sum.send()
     *late, _ = attention_gradient(
@@ -1301,15 +1313,15 @@
         sums=[early_sums],
     )
     late_sum = Sum(links, late, direct=True)
-    early_sum.hold(late[2])
-    up_sum.hold(late[2])
-    up_mine = up_sum.finish()
-    given = after(resid1, late_sum.prepare(), early_sum.prepare(), up_mine)
+    down_sum.hold(late[2])
+    down_mine = down_sum.finish()
+    given = after(resid1, late_sum.prepare(), down_mine)
     late_sum.send()
-    early_sum.send()
     input_grad = input_gradient(links, table, back, given, qkv, qkv_piece)
     late_sum.hold(input_grad)
     early_sum.hold(input_grad)
+    up_sum.hold(input_grad)
+    up_mine = up_sum.finish()
     down_grad = both_halves(links, down_mine, links.swap(down_mine))
     up_grad = both_halves(links, up_mine, links.swap(up_mine))
     early = settle(links, early_sum)

time: 235 us -> 225 us (0.957)
  starting transfers between devices: 44.6 us -> 36.9 us
    ppermute x32 -> x31, starting transfers between devices: 41.6 us -> 34.5 us  [hop(): return lax.ppermute(value, ('ctx', 'dp'), pairs)]
    ppermute x32 -> x31, waiting for transfers between devices: 64 us -> 62.7 us  [hop(): return lax.ppermute(value, ('ctx', 'dp'), pairs)]
    unnamed x44 -> x41, local copies, waits for them, and re-layouts: 5.16 us -> 4.27 us
  transfers between devices with their start and end apart: 53 -> 52, of which waited for: 26 -> 28; matrix products, arithmetic and copies ran while one was open for 2% -> 3% of each run, Pallas kernels for 42% -> 39%
where the time goes in v1:
time: 225 us
  Pallas kernels  101 us (45%)
  waiting for transfers between devices  71.7 us (32%)
  starting transfers between devices  36.9 us (16%)
  local copies, waits for them, and re-layouts  10.1 us (4%)
  other arithmetic  3.6 us (2%)
    pallas_call x13, Pallas kernels, call(): pl.pallas_call(body, name=name, out_shape=outs, in_specs=in_specs, out_sp...  63 us
    ppermute x31, waiting for transfers between devices, hop(): return lax.ppermute(value, ('ctx', 'dp'), pairs)  62.7 us
    ppermute x31, starting transfers between devices, hop(): return lax.ppermute(value, ('ctx', 'dp'), pairs)  34.5 us
    pallas_call x3, Pallas kernels, attend_back(): pl.pallas_call(body, name='attend_back', cost_estimate=cost(5), out_shape...  19 us
    pallas_call x3, Pallas kernels, attend(): pl.pallas_call(body, name='attend', cost_estimate=cost(8), out_shape=[in_...  18.7 us
    ppermute x21, waiting for transfers between devices, swap(): return lax.ppermute(value, 'ctx', [(i, i ^ 1) for i in range(self.ctx)])  8.96 us
  transfers between devices with their start and end apart: 52, of which 28 were waited for; matrix products, arithmetic and copies ran while one was open for 3% of the time, Pallas kernels for 39%

profile of v1, /device:TPU:0, one launch (start us, length us, event | category | flops | bytes accessed | tf_op | source)
XLA Modules:
  0.0 224.9 jit_solution(7494390821922069940)
XLA Ops:
  3.4 5.1 %collective-permute-start.2 = (bf16[48,1280]{1,0:T(8,128)(2,1)S(1)}, bf16[48,1280]{1,0:T(8,128)(2,1)S(1)}, u32[]{:S(2)}, u32[]{:S(2)}) collective-permute-start(bf16[48,1280]{1,0:T(8,128)(2,1)S(1)} %get-tuple-element.264), channel_id=1, source_target_pairs={{0,12},{1,13},{2,14},{3,15},{4,8},{5,9},{6,10},{7,11},{8,4},{9,5},... | collective-permute-start | bytes 368648 | tf_op jit(solution)/shard_map/ppermute | solution.py:50
  21.5 6.4 %collective-permute-done.6 = bf16[192,1280]{1,0:T(8,128)(2,1)S(1)} collective-permute-done((bf16[192,1280]{1,0:T(8,128)(2,1)S(1)}, bf16[192,1280]{1,0:T(8,128)(2,1)S(1)}, u32[]{:S(2)}, u32[]{:S(2)}) %collective-permute-start.6) | collective-permute-done | bytes 491552 | tf_op jit(solution)/shard_map/ppermute | solution.py:50
  33.0 6.2 %collective-permute-done.4 = bf16[48,1920]{1,0:T(8,128)(2,1)S(1)} collective-permute-done((bf16[48,1920]{1,0:T(8,128)(2,1)S(1)}, bf16[48,1920]{1,0:T(8,128)(2,1)S(1)}, u32[]{:S(2)}, u32[]{:S(2)}) %collective-permute-start.4) | collective-permute-done | bytes 184352 | tf_op jit(solution)/shard_map/ppermute | solution.py:50
  48.5 4.9 %qkv.1 = (bf16[512,768]{1,0:T(8,128)(2,1)S(1)}, bf16[512,1536]{1,0:T(8,128)(2,1)S(1)}, f32[16,768]{1,0:T(8,128)S(1)}, f32[1,3072]{1,0:T(1,128)S(1)}, bf16[768,512]{1,0:T(8,128)(2,1)}) custom-call(s32[67]{0:T(128)S(1)} %concatenate.42.scalar, bf16[512,768]{1,0:T(8,128)(2,1)S(1)} %bitcast.34, bf16[384,1280]{1,0:T(8,128)(2,1)} %copy-done.15, ...), custom_call_target="tpu_custom_call" | custom-call | flops 2000000000 | bytes 6000000 | tf_op jit(solution)/shard_map/qkv/pallas_call | solution.py:228
  53.4 4.0 %collective-permute-done.12 = bf16[192,1920]{1,0:T(8,128)(2,1)} collective-permute-done((bf16[192,1920]{1,0:T(8,128)(2,1)S(1)}, bf16[192,1920]{1,0:T(8,128)(2,1)}, u32[]{:S(2)}, u32[]{:S(2)}) %collective-permute-start.12) | collective-permute-done | bytes 737312 | tf_op jit(solution)/shard_map/ppermute | solution.py:50
  65.5 6.2 %attend.3 = (f32[256,512]{1,0:T(8,128)}, bf16[512,256]{1,0:T(8,128)(2,1)S(1)}, bf16[2,1024,1024]{2,1,0:T(8,128)(2,1)}, f32[2,1,1024]{2,1,0:T(1,128)}) custom-call(s32[3]{0:T(128)S(1)} %pad_add_fusion.scalar, bf16[512,768]{1,0:T(8,128)(2,1)S(1)} %copy-done.3, bf16[512,1536]{1,0:T(8,128)(2,1)S(1)} %get-tuple-element.148.refs_0_.refs_1_, ...), custom_call_target="tpu_custom_call" | custom-call | flops 3200000000 | bytes 9600000 | tf_op jit(solution)/shard_map/attend/pallas_call | solution.py:479
  71.8 6.2 %attend.4 = (f32[256,512]{1,0:T(8,128)}, bf16[512,256]{1,0:T(8,128)(2,1)S(1)}, bf16[2,1024,1024]{2,1,0:T(8,128)(2,1)}, f32[2,1,1024]{2,1,0:T(1,128)}) custom-call(s32[3]{0:T(128)S(1)} %pad_add_fusion.scalar, bf16[512,768]{1,0:T(8,128)(2,1)S(1)} %copy-done.3, bf16[512,1536]{1,0:T(8,128)(2,1)S(1)} %get-tuple-element.148.refs_0_.refs_1_, ...), custom_call_target="tpu_custom_call" | custom-call | flops 3200000000 | bytes 9600000 | tf_op jit(solution)/shard_map/attend/pallas_call | solution.py:479
  81.2 6.2 %attend.5 = (f32[256,512]{1,0:T(8,128)}, bf16[512,256]{1,0:T(8,128)(2,1)S(1)}, bf16[2,1024,1024]{2,1,0:T(8,128)(2,1)}, f32[2,1,1024]{2,1,0:T(1,128)}) custom-call(s32[3]{0:T(128)S(1)} %pad_add_fusion.scalar, bf16[512,768]{1,0:T(8,128)(2,1)S(1)} %copy-done.3, bf16[512,1536]{1,0:T(8,128)(2,1)S(1)} %get-tuple-element.148.refs_0_.refs_1_, ...), custom_call_target="tpu_custom_call" | custom-call | flops 3200000000 | bytes 9600000 | tf_op jit(solution)/shard_map/attend/pallas_call | solution.py:479
  91.4 4.4 %after_attention.1 = (f32[512,768]{1,0:T(8,128)S(1)}, bf16[512,768]{1,0:T(8,128)(2,1)S(1)}, bf16[768,512]{1,0:T(8,128)(2,1)S(1)}, bf16[768,512]{1,0:T(8,128)(2,1...) custom-call(s32[67]{0:T(128)S(1)} %concatenate.42.scalar, ...), custom_call_target="tpu_custom_call" | custom-call | flops 1400000000 | bytes 4200000 | tf_op jit(solution)/shard_map/after_attention/pallas_call | solution.py:228
  95.8 8.6 %feed_up.1 = (bf16[512,3072]{1,0:T(8,128)(2,1)S(1)}, bf16[3072,512]{1,0:T(8,128)(2,1)S(1)}, bf16[512,3072]{1,0:T(8,128)(2,1)S(1)}) custom-call(s32[67]{0:T(128)S(1)} %concatenate.42.scalar, bf16[512,768]{1,0:T(8,128)(2,1)S(1)} %get-tuple-element.162.low_ref, f32[1,3072]{1,0:T(1,128)S(1)} %get-tuple-element.163.bias_ref, ...), custom_call_target="tpu_custom_call" | custom-call | flops 3200000000 | bytes 9600000 | tf_op jit(solution)/shard_map/feed_up/pallas_call | solution.py:228
  109.9 8.1 %feed_down.1 = (bf16[512,768]{1,0:T(8,128)(2,1)}, f32[512,768]{1,0:T(8,128)S(1)}, bf16[512,768]{1,0:T(8,128)(2,1)S(1)}, bf16[512,384]{1,0:T(8,128)(2,1)S(1)}, bf...) custom-call(s32[67]{0:T(128)S(1)} %concatenate.42.scalar, bf16[512,3072]{1,0:T(8,128)(2,1)S(1)} %get-tuple-element.164.act_ref, ...), custom_call_target="tpu_custom_call" | custom-call | flops 2400000000 | bytes 7200000 | tf_op jit(solution)/shard_map/feed_down/pallas_call | solution.py:228
  119.8 4.8 %down_gradient.1 = (bf16[768,384]{1,0:T(8,128)(2,1)S(1)}, bf16[768,384]{1,0:T(8,128)(2,1)S(1)}, bf16[1536,384]{1,0:T(8,128)(2,1)S(1)}) custom-call(s32[67]{0:T(128)S(1)} %concatenate.42.scalar, bf16[3072,512]{1,0:T(8,128)(2,1)S(1)} %get-tuple-element.173.lm, bf16[3072,512]{1,0:T(8,128)(2,1)S(1)} %collective-permute-done.21.lt, ...), custom_call_target="tpu_custom_call" | custom-call | flops 2000000000 | bytes 6000000 | tf_op jit(solution)/shard_map/down_gradient/pallas_call | solution.py:228
  124.6 6.2 %feed_back.2 = (f32[512,768]{1,0:T(8,128)S(1)}, bf16[512,1536]{1,0:T(8,128)(2,1)S(1)}, f32[1,1536]{1,0:T(1,128)S(1)}) custom-call(s32[67]{0:T(128)S(1)} %concatenate.42.scalar, bf16[512,3072]{1,0:T(8,128)(2,1)S(1)} %get-tuple-element.170.slope_ref, f32[512,768]{1,0:T(8,128)S(1)} %get-tuple-element.177.so_far_ref, ...), custom_call_target="tpu_custom_call" | custom-call | flops 4000000 | bytes 12000 | tf_op jit(solution)/shard_map/feed_back/pallas_call | solution.py:228
  131.9 6.2 %feed_back.3 = (f32[512,768]{1,0:T(8,128)S(1)}, bf16[512,1536]{1,0:T(8,128)(2,1)S(1)}, f32[1,1536]{1,0:T(1,128)S(1)}) custom-call(s32[67]{0:T(128)S(1)} %concatenate.42.scalar, bf16[512,3072]{1,0:T(8,128)(2,1)S(1)} %get-tuple-element.170.slope_ref, f32[512,768]{1,0:T(8,128)S(1)} %get-tuple-element.179.so_far_ref, ...), custom_call_target="tpu_custom_call" | custom-call | flops 4000000 | bytes 12000 | tf_op jit(solution)/shard_map/feed_back/pallas_call | solution.py:228
  138.1 3.8 %up_gradient.1 = (bf16[192,1536]{1,0:T(8,128)(2,1)S(1)}, bf16[192,1536]{1,0:T(8,128)(2,1)S(1)}, bf16[384,1536]{1,0:T(8,128)(2,1)S(1)}) custom-call(s32[67]{0:T(128)S(1)} %concatenate.42.scalar, bf16[768,512]{1,0:T(8,128)(2,1)S(1)} %get-tuple-element.181.lm, bf16[768,512]{1,0:T(8,128)(2,1)S(1)} %collective-permute-done.23.lt, ...), custom_call_target="tpu_custom_call" | custom-call | flops 2000000000 | bytes 6000000 | tf_op jit(solution)/shard_map/up_gradient/pallas_call | solution.py:228
  143.6 4.0 %collective-permute-done.25 = bf16[1536,384]{1,0:T(8,128)(2,1)S(1)} collective-permute-done((bf16[1536,384]{1,0:T(8,128)(2,1)S(1)}, bf16[1536,384]{1,0:T(8,128)(2,1)S(1)}, u32[]{:S(2)}, u32[]{:S(2)}) %collective-permute-start.25) | collective-permute-done | bytes 1179680 | tf_op jit(solution)/shard_map/ppermute | solution.py:50
  152.2 6.3 %attend_back.3 = (bf16[3584,128]{1,0:T(8,128)(2,1)S(1)}, bf16[1536,128]{1,0:T(8,128)(2,1)S(1)}) custom-call(s32[1]{0:T(128)} %bitcast._, bf16[512,768]{1,0:T(8,128)(2,1)S(1)} %copy-done.4, bf16[512,768]{1,0:T(8,128)(2,1)S(1)} %get-tuple-element.193.gm_ref, f32[256,512]{1,0:T(8,128)} %get-tuple-element.195.mt_ref, ...), custom_call_target="tpu_custom_call" | custom-call | flops 2000000000 | bytes 6000000 | tf_op jit(solution)/shard_map/attend_back/pallas_call | solution.py:595
  158.6 6.5 %attend_back.4 = (bf16[3584,128]{1,0:T(8,128)(2,1)S(1)}, bf16[1536,128]{1,0:T(8,128)(2,1)S(1)}) custom-call(s32[1]{0:T(128)} %bitcast._, bf16[512,768]{1,0:T(8,128)(2,1)S(1)} %copy-done.4, bf16[512,768]{1,0:T(8,128)(2,1)S(1)} %get-tuple-element.193.gm_ref, f32[256,512]{1,0:T(8,128)} %get-tuple-element.200.mt_ref, ...), custom_call_target="tpu_custom_call" | custom-call | flops 2000000000 | bytes 6000000 | tf_op jit(solution)/shard_map/attend_back/pallas_call | solution.py:595
  170.0 3.5 %early_gradient.1 = (bf16[192,1152]{1,0:T(8,128)(2,1)S(1)}, bf16[192,1152]{1,0:T(8,128)(2,1)S(1)}, bf16[384,1152]{1,0:T(8,128)(2,1)S(1)}, f32[2,384]{1,0:T(2,128)S(1)}) custom-call(s32[67]{0:T(128)S(1)} %concatenate.42.scalar, bf16[768,512]{1,0:T(8,128)(2,1)S(1)} %copy-done.6, bf16[768,512]{1,0:T(8,128)(2,1)S(1)} %collective-permute-done.28.xt, ...), custom_call_target="tpu_custom_call" | custom-call | flops 2000000000 | bytes 6000000 | tf_op jit(solution)/shard_map/early_gradient/pallas_call | solution.py:228
  174.1 4.0 %collective-permute-done.34 = bf16[384,384]{1,0:T(8,128)(2,1)S(1)} collective-permute-done((bf16[384,384]{1,0:T(8,128)(2,1)S(1)}, bf16[384,384]{1,0:T(8,128)(2,1)S(1)}, u32[]{:S(2)}, u32[]{:S(2)}) %collective-permute-start.34) | collective-permute-done | bytes 294944 | tf_op jit(solution)/shard_map/ppermute | solution.py:50
  180.7 6.2 %attend_back.5 = (bf16[3584,128]{1,0:T(8,128)(2,1)S(1)}, bf16[1536,128]{1,0:T(8,128)(2,1)S(1)}) custom-call(s32[1]{0:T(128)} %bitcast._, bf16[512,768]{1,0:T(8,128)(2,1)S(1)} %copy-done.4, bf16[512,768]{1,0:T(8,128)(2,1)S(1)} %get-tuple-element.193.gm_ref, f32[256,512]{1,0:T(8,128)} %get-tuple-element.219.mt_ref, ...), custom_call_target="tpu_custom_call" | custom-call | flops 2000000000 | bytes 6000000 | tf_op jit(solution)/shard_map/attend_back/pallas_call | solution.py:595
  195.9 5.8 %input_gradient.1 = f32[512,768]{1,0:T(8,128)} custom-call(s32[67]{0:T(128)S(1)} %concatenate.42.scalar, f32[512,768]{1,0:T(8,128)S(1)} %get-tuple-element.237.resid_ref, bf16[3584,128]{1,0:T(8,128)(2,1)S(1)} %get-tuple-element.208.refs_0_, bf16[1536,128]{1,0:T(8,128)(2,1)S(1)} %get-tuple-element.198.refs_1_, ...), custom_call_target="tpu_custom_call" | custom-call | flops 8000000000 | bytes 24000000 | tf_op jit(solution)/shard_map/input_gradient/pallas_call | solution.py:228
  205.3 5.1 %collective-permute-done.40 = bf16[96,1152]{1,0:T(8,128)(2,1)S(1)} collective-permute-done((bf16[96,1152]{1,0:T(8,128)(2,1)S(1)}, bf16[96,1152]{1,0:T(8,128)(2,1)S(1)}, u32[]{:S(2)}, u32[]{:S(2)}) %collective-permute-start.40) | collective-permute-done | bytes 221216 | tf_op jit(solution)/shard_map/ppermute | solution.py:50
  216.0 4.5 %collective-permute-done.41 = bf16[48,1152]{1,0:T(8,128)(2,1)S(1)} collective-permute-done((bf16[48,1152]{1,0:T(8,128)(2,1)S(1)}, bf16[48,1152]{1,0:T(8,128)(2,1)S(1)}, u32[]{:S(2)}, u32[]{:S(2)}) %collective-permute-start.41) | collective-permute-done | bytes 110624 | tf_op jit(solution)/shard_map/ppermute | solution.py:50
  (180 shorter events, 89.6 us)
Async XLA Ops:
  8.6 10.4 %collective-permute-start = (bf16[48,1280]{1,0:T(8,128)(2,1)S(1)}, bf16[48,1280]{1,0:T(8,128)(2,1)S(1)}, u32[]{:S(2)}, u32[]{:S(2)}) collective-permute-start(bf16[48,1280]{1,0:T(8,128)(2,1)S(1)} %get-tuple-element.264), channel_id=1, source_target_pairs={{0,8},{1,9},{2,10},{3,11},{4,12},{5,13},{6,14},{7,15},{8,0},{9,1},... | collective-permute-start | bytes 368648 | tf_op jit(solution)/shard_map/ppermute | solution.py:50
  20.5 10.3 %collective-permute-start.3 = (bf16[48,1920]{1,0:T(8,128)(2,1)S(1)}, bf16[48,1920]{1,0:T(8,128)(2,1)S(1)}, u32[]{:S(2)}, u32[]{:S(2)}) collective-permute-start(bf16[48,1920]{1,0:T(8,128)(2,1)S(1)} %pad_maximum_fusion.2), channel_id=1, source_target_pairs={{0,8},{1,9},{2,10},{3,11},{4,12},{5,13},{6,14},{7,15},{8,0},{9,1},... | collective-permute-start | bytes 552968 | tf_op jit(solution)/shard_map/ppermute | solution.py:50
  30.8 11.3 %collective-permute-start.7 = (bf16[384,1280]{1,0:T(8,128)(2,1)S(1)}, bf16[384,1280]{1,0:T(8,128)(2,1)S(1)}, u32[]{:S(2)}, u32[]{:S(2)}) collective-permute-start(bf16[384,1280]{1,0:T(8,128)(2,1)S(1)} %constant_dynamic-update-slice_fusion.refs_0_.refs_9_), channel_id=1, source_target_pairs={{0,16},{16,0},{1,17},{17,1},{2,18},{18,2},{3,19},{19,3},{4,20},{20... | collective-permute-start | bytes 2949128 | tf_op jit(solution)/shard_map/ppermute | solution.py:43
  30.8 14.2 %collective-permute-start.8 = (bf16[384,1280]{1,0:T(8,128)(2,1)S(1)}, bf16[384,1280]{1,0:T(8,128)(2,1)}, u32[]{:S(2)}, u32[]{:S(2)}) collective-permute-start(bf16[384,1280]{1,0:T(8,128)(2,1)S(1)} %constant_dynamic-update-slice_fusion.refs_0_.refs_9_), channel_id=1, source_target_pairs={{0,2},{1,3},{2,0},{3,1},{4,6},{5,7},{6,4},{7,5},{8,10},{9,11},{10,... | collective-permute-start | bytes 2949128 | tf_op jit(solution)/shard_map/ppermute | solution.py:50
  31.3 10.8 %collective-permute-start.5 = (bf16[48,1920]{1,0:T(8,128)(2,1)S(1)}, bf16[48,1920]{1,0:T(8,128)(2,1)S(1)}, u32[]{:S(2)}, u32[]{:S(2)}) collective-permute-start(bf16[48,1920]{1,0:T(8,128)(2,1)S(1)} %pad_maximum_fusion.2), channel_id=1, source_target_pairs={{0,12},{1,13},{2,14},{3,15},{4,8},{5,9},{6,10},{7,11},{8,4},{9,5},... | collective-permute-start | bytes 552968 | tf_op jit(solution)/shard_map/ppermute | solution.py:50
  45.8 11.6 %collective-permute-start.12 = (bf16[192,1920]{1,0:T(8,128)(2,1)S(1)}, bf16[192,1920]{1,0:T(8,128)(2,1)}, u32[]{:S(2)}, u32[]{:S(2)}) collective-permute-start(bf16[192,1920]{1,0:T(8,128)(2,1)S(1)} %pad_maximum_fusion), channel_id=1, source_target_pairs={{0,1},{1,0},{2,3},{3,2},{4,5},{5,4},{6,7},{7,6},{8,9},{9,8},{10,11... | collective-permute-start | bytes 2211848 | tf_op jit(solution)/shard_map/ppermute | solution.py:50
  47.5 12.0 %collective-permute-start.9 = (bf16[192,384]{1,0:T(8,128)(2,1)S(1)}, bf16[192,384]{1,0:T(8,128)(2,1)S(1)}, u32[]{:S(2)}, u32[]{:S(2)}) collective-permute-start(bf16[192,384]{1,0:T(8,128)(2,1)S(1)} %constant_dynamic-slice_fusion.3), channel_id=1, source_target_pairs={{0,8},{1,9},{2,10},{3,11},{4,12},{5,13},{6,14},{7,15},{8,0},{9,1},... | collective-permute-start | bytes 442376 | tf_op jit(solution)/shard_map/ppermute | solution.py:50
  59.4 18.6 %collective-permute-start.15 = (bf16[384,1920]{1,0:T(8,128)(2,1)}, bf16[384,1920]{1,0:T(8,128)(2,1)}, u32[]{:S(2)}, u32[]{:S(2)}) collective-permute-start(bf16[384,1920]{1,0:T(8,128)(2,1)} %constant_dynamic-update-slice_fusion.7.refs_3_.refs_0_.um), channel_id=1, source_target_pairs={{0,16},{16,0},{1,17},{17,1},{2,18},{18,2},{3,19},{19,3},{4,20},{20... | collective-permute-start | bytes 4423688 | tf_op jit(solution)/shard_map/ppermute | solution.py:43
  60.0 19.7 %collective-permute-start.16 = (bf16[384,1920]{1,0:T(8,128)(2,1)}, bf16[384,1920]{1,0:T(8,128)(2,1)}, u32[]{:S(2)}, u32[]{:S(2)}) collective-permute-start(bf16[384,1920]{1,0:T(8,128)(2,1)} %constant_dynamic-update-slice_fusion.7.refs_3_.refs_0_.um), channel_id=1, source_target_pairs={{0,2},{1,3},{2,0},{3,1},{4,6},{5,7},{6,4},{7,5},{8,10},{9,11},{10,... | collective-permute-start | bytes 4423688 | tf_op jit(solution)/shard_map/ppermute | solution.py:50
  60.6 11.1 %collective-permute-start.11 = (bf16[384,384]{1,0:T(8,128)(2,1)S(1)}, bf16[384,384]{1,0:T(8,128)(2,1)S(1)}, u32[]{:S(2)}, u32[]{:S(2)}) collective-permute-start(bf16[384,384]{1,0:T(8,128)(2,1)S(1)} %constant_dynamic-update-slice_fusion.5), channel_id=1, source_target_pairs={{0,4},{1,5},{2,6},{3,7},{4,0},{5,1},{6,2},{7,3},{8,12},{9,13},{10,... | collective-permute-start | bytes 884744 | tf_op jit(solution)/shard_map/ppermute | solution.py:50
  79.6 10.6 %collective-permute-start.17 = (bf16[384,1920]{1,0:T(8,128)(2,1)}, bf16[384,1920]{1,0:T(8,128)(2,1)S(1)}, u32[]{:S(2)}, u32[]{:S(2)}) collective-permute-start(bf16[384,1920]{1,0:T(8,128)(2,1)} %collective-permute-done.16.refs_4_.refs_1_.ul), channel_id=1, source_target_pairs={{0,16},{16,0},{1,17},{17,1},{2,18},{18,2},{3,19},{19,3},{4,20},{20... | collective-permute-start | bytes 4423688 | tf_op jit(solution)/shard_map/ppermute | solution.py:43
  89.6 14.8 %collective-permute-start.18 = (bf16[1536,384]{1,0:T(8,128)(2,1)S(1)}, bf16[1536,384]{1,0:T(8,128)(2,1)S(1)}, u32[]{:S(2)}, u32[]{:S(2)}) collective-permute-start(bf16[1536,384]{1,0:T(8,128)(2,1)S(1)} %constant_dynamic-update-slice_fusion.11.refs_0_), channel_id=1, source_target_pairs={{0,16},{16,0},{1,17},{17,1},{2,18},{18,2},{3,19},{19,3},{4,20},{20... | collective-permute-start | bytes 3538952 | tf_op jit(solution)/shard_map/ppermute | solution.py:43
  89.7 16.3 %collective-permute-start.19 = (bf16[1536,384]{1,0:T(8,128)(2,1)S(1)}, bf16[1536,384]{1,0:T(8,128)(2,1)S(1)}, u32[]{:S(2)}, u32[]{:S(2)}) collective-permute-start(bf16[1536,384]{1,0:T(8,128)(2,1)S(1)} %constant_dynamic-update-slice_fusion.11.refs_0_), channel_id=1, source_target_pairs={{0,2},{1,3},{2,0},{3,1},{4,6},{5,7},{6,4},{7,5},{8,10},{9,11},{10,... | collective-permute-start | bytes 3538952 | tf_op jit(solution)/shard_map/ppermute | solution.py:50
  108.8 10.9 %collective-permute-start.21 = (bf16[3072,512]{1,0:T(8,128)(2,1)S(1)}, bf16[3072,512]{1,0:T(8,128)(2,1)S(1)}, u32[]{:S(2)}, u32[]{:S(2)}) collective-permute-start(bf16[3072,512]{1,0:T(8,128)(2,1)S(1)} %get-tuple-element.173.lm), channel_id=1, source_target_pairs={{0,16},{16,0},{1,17},{17,1},{2,18},{18,2},{3,19},{19,3},{4,20},{20... | collective-permute-start | bytes 9437192 | tf_op jit(solution)/shard_map/ppermute | solution.py:43
  131.4 16.2 %collective-permute-start.25 = (bf16[1536,384]{1,0:T(8,128)(2,1)S(1)}, bf16[1536,384]{1,0:T(8,128)(2,1)S(1)}, u32[]{:S(2)}, u32[]{:S(2)}) collective-permute-start(bf16[1536,384]{1,0:T(8,128)(2,1)S(1)} %get-tuple-element.176), channel_id=1, source_target_pairs={{0,2},{1,3},{2,0},{3,1},{4,6},{5,7},{6,4},{7,5},{8,10},{9,11},{10,... | collective-permute-start | bytes 3538952 | tf_op jit(solution)/shard_map/ppermute | solution.py:50
  142.0 24.6 %collective-permute-start.27 = (bf16[384,1536]{1,0:T(8,128)(2,1)S(1)}, bf16[384,1536]{1,0:T(8,128)(2,1)S(1)}, u32[]{:S(2)}, u32[]{:S(2)}) collective-permute-start(bf16[384,1536]{1,0:T(8,128)(2,1)S(1)} %get-tuple-element.184), channel_id=1, source_target_pairs={{0,2},{1,3},{2,0},{3,1},{4,6},{5,7},{6,4},{7,5},{8,10},{9,11},{10,... | collective-permute-start | bytes 3538952 | tf_op jit(solution)/shard_map/ppermute | solution.py:50
  143.6 23.1 %collective-permute-start.28 = (bf16[768,512]{1,0:T(8,128)(2,1)S(1)}, bf16[768,512]{1,0:T(8,128)(2,1)S(1)}, u32[]{:S(2)}, u32[]{:S(2)}) collective-permute-start(bf16[768,512]{1,0:T(8,128)(2,1)S(1)} %copy-done.6), channel_id=1, source_target_pairs={{0,16},{16,0},{1,17},{17,1},{2,18},{18,2},{3,19},{19,3},{4,20},{20... | collective-permute-start | bytes 2359304 | tf_op jit(solution)/shard_map/ppermute | solution.py:43
  147.8 20.5 %collective-permute-start.26 = (bf16[768,384]{1,0:T(8,128)(2,1)S(1)}, bf16[768,384]{1,0:T(8,128)(2,1)S(1)}, u32[]{:S(2)}, u32[]{:S(2)}) collective-permute-start(bf16[768,384]{1,0:T(8,128)(2,1)S(1)} %reduce-precision_convert_fusion.1), channel_id=1, source_target_pairs={{0,1},{1,0},{2,3},{3,2},{4,5},{5,4},{6,7},{7,6},{8,9},{9,8},{10,11... | collective-permute-start | bytes 1769480 | tf_op jit(solution)/shard_map/ppermute | solution.py:50
  158.5 11.5 %collective-permute-start.29 = (bf16[3584,128]{1,0:T(8,128)(2,1)S(1)}, bf16[3584,128]{1,0:T(8,128)(2,1)S(1)}, u32[]{:S(2)}, u32[]{:S(2)}) collective-permute-start(bf16[3584,128]{1,0:T(8,128)(2,1)S(1)} %get-tuple-element.208.refs_0_), channel_id=1, source_target_pairs={{0,16},{16,0},{1,17},{17,1},{2,18},{18,2},{3,19},{19,3},{4,20},{20... | collective-permute-start | bytes 2752520 | tf_op jit(solution)/shard_map/ppermute | solution.py:43
  166.7 11.4 %collective-permute-start.35 = (bf16[192,1536]{1,0:T(8,128)(2,1)S(1)}, bf16[192,1536]{1,0:T(8,128)(2,1)S(1)}, u32[]{:S(2)}, u32[]{:S(2)}) collective-permute-start(bf16[192,1536]{1,0:T(8,128)(2,1)S(1)} %reduce-precision_convert_fusion), channel_id=1, source_target_pairs={{0,1},{1,0},{2,3},{3,2},{4,5},{5,4},{6,7},{7,6},{8,9},{9,8},{10,11... | collective-permute-start | bytes 1769480 | tf_op jit(solution)/shard_map/ppermute | solution.py:50
  173.5 14.3 %collective-permute-start.33 = (bf16[384,1152]{1,0:T(8,128)(2,1)S(1)}, bf16[384,1152]{1,0:T(8,128)(2,1)S(1)}, u32[]{:S(2)}, u32[]{:S(2)}) collective-permute-start(bf16[384,1152]{1,0:T(8,128)(2,1)S(1)} %get-tuple-element.214), channel_id=1, source_target_pairs={{0,2},{1,3},{2,0},{3,1},{4,6},{5,7},{6,4},{7,5},{8,10},{9,11},{10,... | collective-permute-start | bytes 2654216 | tf_op jit(solution)/shard_map/ppermute | solution.py:50
  178.2 11.7 %collective-permute-start.36 = (bf16[96,1536]{1,0:T(8,128)(2,1)S(1)}, bf16[96,1536]{1,0:T(8,128)(2,1)S(1)}, u32[]{:S(2)}, u32[]{:S(2)}) collective-permute-start(bf16[96,1536]{1,0:T(8,128)(2,1)S(1)} %reduce-precision_convert_fusion.3), channel_id=1, source_target_pairs={{0,4},{1,5},{2,6},{3,7},{4,0},{5,1},{6,2},{7,3},{8,12},{9,13},{10,... | collective-permute-start | bytes 884744 | tf_op jit(solution)/shard_map/ppermute | solution.py:50
  190.0 12.1 %collective-permute-start.39 = (bf16[192,1152]{1,0:T(8,128)(2,1)S(1)}, bf16[192,1152]{1,0:T(8,128)(2,1)S(1)}, u32[]{:S(2)}, u32[]{:S(2)}) collective-permute-start(bf16[192,1152]{1,0:T(8,128)(2,1)S(1)} %reduce-precision_convert_fusion.2), channel_id=1, source_target_pairs={{0,1},{1,0},{2,3},{3,2},{4,5},{5,4},{6,7},{7,6},{8,9},{9,8},{10,11... | collective-permute-start | bytes 1327112 | tf_op jit(solution)/shard_map/ppermute | solution.py:50
  191.2 10.9 %collective-permute-start.49 = (bf16[48,1536]{1,0:T(8,128)(2,1)S(1)}, bf16[48,1536]{1,0:T(8,128)(2,1)S(1)}, u32[]{:S(2)}, u32[]{:S(2)}) collective-permute-start(bf16[48,1536]{1,0:T(8,128)(2,1)S(1)} %reduce-precision_convert_fusion.9), channel_id=1, source_target_pairs={{0,8},{1,9},{2,10},{3,11},{4,12},{5,13},{6,14},{7,15},{8,0},{9,1},... | collective-permute-start | bytes 442376 | tf_op jit(solution)/shard_map/ppermute | solution.py:50
  (45 other events, 284.6 us)

commit v2 on v1

--- a/solution.py
+++ b/solution.py
@@ -11,8 +11,8 @@
 LANES = 128
 VECTORS = 16
 VMEM_BYTES = 24 << 20
-FLOPS = 400_000_000
-BYTES = 1_200_000
+FLOPS = 300_000_000
+BYTES = 900_000
 
 masked_score = -1e30
 norm_eps = 1e-05
@@ -1312,7 +1312,7 @@
         folds=folds,
         sums=[early_sums],
     )
-    late_sum = Sum(links, late, direct=True)
+    late_sum = Sum(links, late)
     down_sum.hold(late[2])
     down_mine = down_sum.finish()
     given = after(resid1, late_sum.prepare(), down_mine)

time: 225 us -> 223 us (level)
    ppermute x31 -> x30, starting transfers between devices: 34.5 us -> 32.4 us  [hop(): return lax.ppermute(value, ('ctx', 'dp'), pairs)]
    ppermute x31 -> x30, waiting for transfers between devices: 62.7 us -> 61 us  [hop(): return lax.ppermute(value, ('ctx', 'dp'), pairs)]
  transfers between devices with their start and end apart: 52 -> 51, of which waited for: 28 -> 28; matrix products, arithmetic and copies ran while one was open for 3% -> 3% of each run, Pallas kernels for 39% -> 40%
where the time goes in v2:
time: 223 us; the launch traced here: 222 us
  Pallas kernels  101 us (45%)
  waiting for transfers between devices  70.3 us (32%)
  starting transfers between devices  35.3 us (16%)
  local copies, waits for them, and re-layouts  10.1 us (5%)
  other arithmetic  3.62 us (2%)
    pallas_call x13, Pallas kernels, call(): pl.pallas_call(body, name=name, out_shape=outs, in_specs=in_specs, out_sp...  63 us
    ppermute x30, waiting for transfers between devices, hop(): return lax.ppermute(value, ('ctx', 'dp'), pairs)  61 us
    ppermute x30, starting transfers between devices, hop(): return lax.ppermute(value, ('ctx', 'dp'), pairs)  32.4 us
    pallas_call x3, Pallas kernels, attend_back(): pl.pallas_call(body, name='attend_back', cost_estimate=cost(5), out_shape...  19 us
    pallas_call x3, Pallas kernels, attend(): pl.pallas_call(body, name='attend', cost_estimate=cost(8), out_shape=[in_...  18.7 us
    ppermute x21, waiting for transfers between devices, swap(): return lax.ppermute(value, 'ctx', [(i, i ^ 1) for i in range(self.ctx)])  9.35 us
  transfers between devices with their start and end apart: 51, of which 28 were waited for; matrix products, arithmetic and copies ran while one was open for 3% of the time, Pallas kernels for 40%

profile of v2, /device:TPU:0, one launch (start us, length us, event | category | flops | bytes accessed | tf_op | source)
XLA Modules:
  0.0 222.0 jit_solution(4059182382237936611)
XLA Ops:
  3.4 5.1 %collective-permute-start.2 = (bf16[48,1280]{1,0:T(8,128)(2,1)S(1)}, bf16[48,1280]{1,0:T(8,128)(2,1)S(1)}, u32[]{:S(2)}, u32[]{:S(2)}) collective-permute-start(bf16[48,1280]{1,0:T(8,128)(2,1)S(1)} %get-tuple-element.261), channel_id=1, source_target_pairs={{0,12},{1,13},{2,14},{3,15},{4,8},{5,9},{6,10},{7,11},{8,4},{9,5},... | collective-permute-start | bytes 368648 | tf_op jit(solution)/shard_map/ppermute | solution.py:50
  15.6 3.3 %collective-permute-done = bf16[48,1280]{1,0:T(8,128)(2,1)S(1)} collective-permute-done((bf16[48,1280]{1,0:T(8,128)(2,1)S(1)}, bf16[48,1280]{1,0:T(8,128)(2,1)S(1)}, u32[]{:S(2)}, u32[]{:S(2)}) %collective-permute-start) | collective-permute-done | bytes 122912 | tf_op jit(solution)/shard_map/ppermute | solution.py:50
  21.5 6.4 %collective-permute-done.6 = bf16[192,1280]{1,0:T(8,128)(2,1)S(1)} collective-permute-done((bf16[192,1280]{1,0:T(8,128)(2,1)S(1)}, bf16[192,1280]{1,0:T(8,128)(2,1)S(1)}, u32[]{:S(2)}, u32[]{:S(2)}) %collective-permute-start.6) | collective-permute-done | bytes 491552 | tf_op jit(solution)/shard_map/ppermute | solution.py:50
  33.0 6.2 %collective-permute-done.4 = bf16[48,1920]{1,0:T(8,128)(2,1)S(1)} collective-permute-done((bf16[48,1920]{1,0:T(8,128)(2,1)S(1)}, bf16[48,1920]{1,0:T(8,128)(2,1)S(1)}, u32[]{:S(2)}, u32[]{:S(2)}) %collective-permute-start.4) | collective-permute-done | bytes 184352 | tf_op jit(solution)/shard_map/ppermute | solution.py:50
  48.5 4.9 %qkv.1 = (bf16[512,768]{1,0:T(8,128)(2,1)S(1)}, bf16[512,1536]{1,0:T(8,128)(2,1)S(1)}, f32[16,768]{1,0:T(8,128)S(1)}, f32[1,3072]{1,0:T(1,128)S(1)}, bf16[768,512]{1,0:T(8,128)(2,1)}) custom-call(s32[67]{0:T(128)S(1)} %concatenate.42.scalar, bf16[512,768]{1,0:T(8,128)(2,1)S(1)} %bitcast.34, bf16[384,1280]{1,0:T(8,128)(2,1)} %copy-done.15, ...), custom_call_target="tpu_custom_call" | custom-call | flops 1500000000 | bytes 4500000 | tf_op jit(solution)/shard_map/qkv/pallas_call | solution.py:228
  53.3 3.4 %collective-permute-done.12 = bf16[192,1920]{1,0:T(8,128)(2,1)} collective-permute-done((bf16[192,1920]{1,0:T(8,128)(2,1)S(1)}, bf16[192,1920]{1,0:T(8,128)(2,1)}, u32[]{:S(2)}, u32[]{:S(2)}) %collective-permute-start.12) | collective-permute-done | bytes 737312 | tf_op jit(solution)/shard_map/ppermute | solution.py:50
  64.8 6.2 %attend.3 = (f32[256,512]{1,0:T(8,128)}, bf16[512,256]{1,0:T(8,128)(2,1)S(1)}, bf16[2,1024,1024]{2,1,0:T(8,128)(2,1)}, f32[2,1,1024]{2,1,0:T(1,128)}) custom-call(s32[3]{0:T(128)S(1)} %pad_add_fusion.scalar, bf16[512,768]{1,0:T(8,128)(2,1)S(1)} %copy-done.3, bf16[512,1536]{1,0:T(8,128)(2,1)S(1)} %get-tuple-element.148.refs_0_.refs_1_, ...), custom_call_target="tpu_custom_call" | custom-call | flops 2400000000 | bytes 7200000 | tf_op jit(solution)/shard_map/attend/pallas_call | solution.py:479
  71.1 6.2 %attend.4 = (f32[256,512]{1,0:T(8,128)}, bf16[512,256]{1,0:T(8,128)(2,1)S(1)}, bf16[2,1024,1024]{2,1,0:T(8,128)(2,1)}, f32[2,1,1024]{2,1,0:T(1,128)}) custom-call(s32[3]{0:T(128)S(1)} %pad_add_fusion.scalar, bf16[512,768]{1,0:T(8,128)(2,1)S(1)} %copy-done.3, bf16[512,1536]{1,0:T(8,128)(2,1)S(1)} %get-tuple-element.148.refs_0_.refs_1_, ...), custom_call_target="tpu_custom_call" | custom-call | flops 2400000000 | bytes 7200000 | tf_op jit(solution)/shard_map/attend/pallas_call | solution.py:479
  79.0 6.3 %attend.5 = (f32[256,512]{1,0:T(8,128)}, bf16[512,256]{1,0:T(8,128)(2,1)S(1)}, bf16[2,1024,1024]{2,1,0:T(8,128)(2,1)}, f32[2,1,1024]{2,1,0:T(1,128)}) custom-call(s32[3]{0:T(128)S(1)} %pad_add_fusion.scalar, bf16[512,768]{1,0:T(8,128)(2,1)S(1)} %copy-done.3, bf16[512,1536]{1,0:T(8,128)(2,1)S(1)} %get-tuple-element.148.refs_0_.refs_1_, ...), custom_call_target="tpu_custom_call" | custom-call | flops 2400000000 | bytes 7200000 | tf_op jit(solution)/shard_map/attend/pallas_call | solution.py:479
  89.1 4.4 %after_attention.1 = (f32[512,768]{1,0:T(8,128)S(1)}, bf16[512,768]{1,0:T(8,128)(2,1)S(1)}, bf16[768,512]{1,0:T(8,128)(2,1)S(1)}, bf16[768,512]{1,0:T(8,128)(2,1...) custom-call(s32[67]{0:T(128)S(1)} %concatenate.42.scalar, ...), custom_call_target="tpu_custom_call" | custom-call | flops 1050000000 | bytes 3150000 | tf_op jit(solution)/shard_map/after_attention/pallas_call | solution.py:228
  93.5 8.6 %feed_up.1 = (bf16[512,3072]{1,0:T(8,128)(2,1)S(1)}, bf16[3072,512]{1,0:T(8,128)(2,1)S(1)}, bf16[512,3072]{1,0:T(8,128)(2,1)S(1)}) custom-call(s32[67]{0:T(128)S(1)} %concatenate.42.scalar, bf16[512,768]{1,0:T(8,128)(2,1)S(1)} %get-tuple-element.162.low_ref, f32[1,3072]{1,0:T(1,128)S(1)} %get-tuple-element.163.bias_ref, ...), custom_call_target="tpu_custom_call" | custom-call | flops 2400000000 | bytes 7200000 | tf_op jit(solution)/shard_map/feed_up/pallas_call | solution.py:228
  107.6 8.1 %feed_down.1 = (bf16[512,768]{1,0:T(8,128)(2,1)}, f32[512,768]{1,0:T(8,128)S(1)}, bf16[512,768]{1,0:T(8,128)(2,1)S(1)}, bf16[512,384]{1,0:T(8,128)(2,1)S(1)}, bf...) custom-call(s32[67]{0:T(128)S(1)} %concatenate.42.scalar, bf16[512,3072]{1,0:T(8,128)(2,1)S(1)} %get-tuple-element.164.act_ref, ...), custom_call_target="tpu_custom_call" | custom-call | flops 1800000000 | bytes 5400000 | tf_op jit(solution)/shard_map/feed_down/pallas_call | solution.py:228
  117.5 4.8 %down_gradient.1 = (bf16[768,384]{1,0:T(8,128)(2,1)S(1)}, bf16[768,384]{1,0:T(8,128)(2,1)S(1)}, bf16[1536,384]{1,0:T(8,128)(2,1)S(1)}) custom-call(s32[67]{0:T(128)S(1)} %concatenate.42.scalar, bf16[3072,512]{1,0:T(8,128)(2,1)S(1)} %get-tuple-element.173.lm, bf16[3072,512]{1,0:T(8,128)(2,1)S(1)} %collective-permute-done.21.lt, ...), custom_call_target="tpu_custom_call" | custom-call | flops 1500000000 | bytes 4500000 | tf_op jit(solution)/shard_map/down_gradient/pallas_call | solution.py:228
  122.3 6.2 %feed_back.2 = (f32[512,768]{1,0:T(8,128)S(1)}, bf16[512,1536]{1,0:T(8,128)(2,1)S(1)}, f32[1,1536]{1,0:T(1,128)S(1)}) custom-call(s32[67]{0:T(128)S(1)} %concatenate.42.scalar, bf16[512,3072]{1,0:T(8,128)(2,1)S(1)} %get-tuple-element.170.slope_ref, f32[512,768]{1,0:T(8,128)S(1)} %get-tuple-element.177.so_far_ref, ...), custom_call_target="tpu_custom_call" | custom-call | flops 3000000 | bytes 9000 | tf_op jit(solution)/shard_map/feed_back/pallas_call | solution.py:228
  129.6 6.2 %feed_back.3 = (f32[512,768]{1,0:T(8,128)S(1)}, bf16[512,1536]{1,0:T(8,128)(2,1)S(1)}, f32[1,1536]{1,0:T(1,128)S(1)}) custom-call(s32[67]{0:T(128)S(1)} %concatenate.42.scalar, bf16[512,3072]{1,0:T(8,128)(2,1)S(1)} %get-tuple-element.170.slope_ref, f32[512,768]{1,0:T(8,128)S(1)} %get-tuple-element.179.so_far_ref, ...), custom_call_target="tpu_custom_call" | custom-call | flops 3000000 | bytes 9000 | tf_op jit(solution)/shard_map/feed_back/pallas_call | solution.py:228
  135.8 3.8 %up_gradient.1 = (bf16[192,1536]{1,0:T(8,128)(2,1)S(1)}, bf16[192,1536]{1,0:T(8,128)(2,1)S(1)}, bf16[384,1536]{1,0:T(8,128)(2,1)S(1)}) custom-call(s32[67]{0:T(128)S(1)} %concatenate.42.scalar, bf16[768,512]{1,0:T(8,128)(2,1)S(1)} %get-tuple-element.181.lm, bf16[768,512]{1,0:T(8,128)(2,1)S(1)} %collective-permute-done.23.lt, ...), custom_call_target="tpu_custom_call" | custom-call | flops 1500000000 | bytes 4500000 | tf_op jit(solution)/shard_map/up_gradient/pallas_call | solution.py:228
  141.8 3.5 %collective-permute-done.25 = bf16[1536,384]{1,0:T(8,128)(2,1)S(1)} collective-permute-done((bf16[1536,384]{1,0:T(8,128)(2,1)S(1)}, bf16[1536,384]{1,0:T(8,128)(2,1)S(1)}, u32[]{:S(2)}, u32[]{:S(2)}) %collective-permute-start.25) | collective-permute-done | bytes 1179680 | tf_op jit(solution)/shard_map/ppermute | solution.py:50
  149.9 6.3 %attend_back.3 = (bf16[3584,128]{1,0:T(8,128)(2,1)S(1)}, bf16[1536,128]{1,0:T(8,128)(2,1)S(1)}) custom-call(s32[1]{0:T(128)} %bitcast._, bf16[512,768]{1,0:T(8,128)(2,1)S(1)} %copy-done.4, bf16[512,768]{1,0:T(8,128)(2,1)S(1)} %get-tuple-element.193.gm_ref, f32[256,512]{1,0:T(8,128)} %get-tuple-element.195.mt_ref, ...), custom_call_target="tpu_custom_call" | custom-call | flops 1500000000 | bytes 4500000 | tf_op jit(solution)/shard_map/attend_back/pallas_call | solution.py:595
  156.3 6.5 %attend_back.4 = (bf16[3584,128]{1,0:T(8,128)(2,1)S(1)}, bf16[1536,128]{1,0:T(8,128)(2,1)S(1)}) custom-call(s32[1]{0:T(128)} %bitcast._, bf16[512,768]{1,0:T(8,128)(2,1)S(1)} %copy-done.4, bf16[512,768]{1,0:T(8,128)(2,1)S(1)} %get-tuple-element.193.gm_ref, f32[256,512]{1,0:T(8,128)} %get-tuple-element.200.mt_ref, ...), custom_call_target="tpu_custom_call" | custom-call | flops 1500000000 | bytes 4500000 | tf_op jit(solution)/shard_map/attend_back/pallas_call | solution.py:595
  167.7 3.5 %early_gradient.1 = (bf16[192,1152]{1,0:T(8,128)(2,1)S(1)}, bf16[192,1152]{1,0:T(8,128)(2,1)S(1)}, bf16[384,1152]{1,0:T(8,128)(2,1)S(1)}, f32[2,384]{1,0:T(2,128)S(1)}) custom-call(s32[67]{0:T(128)S(1)} %concatenate.42.scalar, bf16[768,512]{1,0:T(8,128)(2,1)S(1)} %copy-done.6, bf16[768,512]{1,0:T(8,128)(2,1)S(1)} %collective-permute-done.28.xt, ...), custom_call_target="tpu_custom_call" | custom-call | flops 1500000000 | bytes 4500000 | tf_op jit(solution)/shard_map/early_gradient/pallas_call | solution.py:228
  171.8 3.8 %collective-permute-done.34 = bf16[384,384]{1,0:T(8,128)(2,1)S(1)} collective-permute-done((bf16[384,384]{1,0:T(8,128)(2,1)S(1)}, bf16[384,384]{1,0:T(8,128)(2,1)S(1)}, u32[]{:S(2)}, u32[]{:S(2)}) %collective-permute-start.34) | collective-permute-done | bytes 294944 | tf_op jit(solution)/shard_map/ppermute | solution.py:50
  178.3 6.2 %attend_back.5 = (bf16[3584,128]{1,0:T(8,128)(2,1)S(1)}, bf16[1536,128]{1,0:T(8,128)(2,1)S(1)}) custom-call(s32[1]{0:T(128)} %bitcast._, bf16[512,768]{1,0:T(8,128)(2,1)S(1)} %copy-done.4, bf16[512,768]{1,0:T(8,128)(2,1)S(1)} %get-tuple-element.193.gm_ref, f32[256,512]{1,0:T(8,128)} %get-tuple-element.219.mt_ref, ...), custom_call_target="tpu_custom_call" | custom-call | flops 1500000000 | bytes 4500000 | tf_op jit(solution)/shard_map/attend_back/pallas_call | solution.py:595
  193.2 5.8 %input_gradient.1 = f32[512,768]{1,0:T(8,128)} custom-call(s32[67]{0:T(128)S(1)} %concatenate.42.scalar, f32[512,768]{1,0:T(8,128)S(1)} %get-tuple-element.237.resid_ref, bf16[3584,128]{1,0:T(8,128)(2,1)S(1)} %get-tuple-element.208.refs_0_, bf16[1536,128]{1,0:T(8,128)(2,1)S(1)} %get-tuple-element.198.refs_1_, ...), custom_call_target="tpu_custom_call" | custom-call | flops 6000000000 | bytes 18000000 | tf_op jit(solution)/shard_map/input_gradient/pallas_call | solution.py:228
  202.7 4.7 %collective-permute-done.44 = bf16[192,512]{1,0:T(8,128)(2,1)S(1)} collective-permute-done((bf16[192,512]{1,0:T(8,128)(2,1)S(1)}, bf16[192,512]{1,0:T(8,128)(2,1)S(1)}, u32[]{:S(2)}, u32[]{:S(2)}) %collective-permute-start.44) | collective-permute-done | bytes 196640 | tf_op jit(solution)/shard_map/ppermute | solution.py:50
  (179 shorter events, 89.5 us)
Async XLA Ops:
  8.6 10.4 %collective-permute-start = (bf16[48,1280]{1,0:T(8,128)(2,1)S(1)}, bf16[48,1280]{1,0:T(8,128)(2,1)S(1)}, u32[]{:S(2)}, u32[]{:S(2)}) collective-permute-start(bf16[48,1280]{1,0:T(8,128)(2,1)S(1)} %get-tuple-element.261), channel_id=1, source_target_pairs={{0,8},{1,9},{2,10},{3,11},{4,12},{5,13},{6,14},{7,15},{8,0},{9,1},... | collective-permute-start | bytes 368648 | tf_op jit(solution)/shard_map/ppermute | solution.py:50
  20.5 10.3 %collective-permute-start.3 = (bf16[48,1920]{1,0:T(8,128)(2,1)S(1)}, bf16[48,1920]{1,0:T(8,128)(2,1)S(1)}, u32[]{:S(2)}, u32[]{:S(2)}) collective-permute-start(bf16[48,1920]{1,0:T(8,128)(2,1)S(1)} %pad_maximum_fusion.2), channel_id=1, source_target_pairs={{0,8},{1,9},{2,10},{3,11},{4,12},{5,13},{6,14},{7,15},{8,0},{9,1},... | collective-permute-start | bytes 552968 | tf_op jit(solution)/shard_map/ppermute | solution.py:50
  30.8 11.3 %collective-permute-start.7 = (bf16[384,1280]{1,0:T(8,128)(2,1)S(1)}, bf16[384,1280]{1,0:T(8,128)(2,1)S(1)}, u32[]{:S(2)}, u32[]{:S(2)}) collective-permute-start(bf16[384,1280]{1,0:T(8,128)(2,1)S(1)} %constant_dynamic-update-slice_fusion.refs_0_.refs_9_), channel_id=1, source_target_pairs={{0,16},{16,0},{1,17},{17,1},{2,18},{18,2},{3,19},{19,3},{4,20},{20... | collective-permute-start | bytes 2949128 | tf_op jit(solution)/shard_map/ppermute | solution.py:43
  30.8 14.2 %collective-permute-start.8 = (bf16[384,1280]{1,0:T(8,128)(2,1)S(1)}, bf16[384,1280]{1,0:T(8,128)(2,1)}, u32[]{:S(2)}, u32[]{:S(2)}) collective-permute-start(bf16[384,1280]{1,0:T(8,128)(2,1)S(1)} %constant_dynamic-update-slice_fusion.refs_0_.refs_9_), channel_id=1, source_target_pairs={{0,2},{1,3},{2,0},{3,1},{4,6},{5,7},{6,4},{7,5},{8,10},{9,11},{10,... | collective-permute-start | bytes 2949128 | tf_op jit(solution)/shard_map/ppermute | solution.py:50
  31.3 10.8 %collective-permute-start.5 = (bf16[48,1920]{1,0:T(8,128)(2,1)S(1)}, bf16[48,1920]{1,0:T(8,128)(2,1)S(1)}, u32[]{:S(2)}, u32[]{:S(2)}) collective-permute-start(bf16[48,1920]{1,0:T(8,128)(2,1)S(1)} %pad_maximum_fusion.2), channel_id=1, source_target_pairs={{0,12},{1,13},{2,14},{3,15},{4,8},{5,9},{6,10},{7,11},{8,4},{9,5},... | collective-permute-start | bytes 552968 | tf_op jit(solution)/shard_map/ppermute | solution.py:50
  45.1 11.6 %collective-permute-start.12 = (bf16[192,1920]{1,0:T(8,128)(2,1)S(1)}, bf16[192,1920]{1,0:T(8,128)(2,1)}, u32[]{:S(2)}, u32[]{:S(2)}) collective-permute-start(bf16[192,1920]{1,0:T(8,128)(2,1)S(1)} %pad_maximum_fusion), channel_id=1, source_target_pairs={{0,1},{1,0},{2,3},{3,2},{4,5},{5,4},{6,7},{7,6},{8,9},{9,8},{10,11... | collective-permute-start | bytes 2211848 | tf_op jit(solution)/shard_map/ppermute | solution.py:50
  47.5 11.3 %collective-permute-start.9 = (bf16[192,384]{1,0:T(8,128)(2,1)S(1)}, bf16[192,384]{1,0:T(8,128)(2,1)S(1)}, u32[]{:S(2)}, u32[]{:S(2)}) collective-permute-start(bf16[192,384]{1,0:T(8,128)(2,1)S(1)} %constant_dynamic-slice_fusion.3), channel_id=1, source_target_pairs={{0,8},{1,9},{2,10},{3,11},{4,12},{5,13},{6,14},{7,15},{8,0},{9,1},... | collective-permute-start | bytes 442376 | tf_op jit(solution)/shard_map/ppermute | solution.py:50
  58.8 20.1 %collective-permute-start.15 = (bf16[384,1920]{1,0:T(8,128)(2,1)}, bf16[384,1920]{1,0:T(8,128)(2,1)}, u32[]{:S(2)}, u32[]{:S(2)}) collective-permute-start(bf16[384,1920]{1,0:T(8,128)(2,1)} %constant_dynamic-update-slice_fusion.7.refs_3_.refs_0_.um), channel_id=1, source_target_pairs={{0,16},{16,0},{1,17},{17,1},{2,18},{18,2},{3,19},{19,3},{4,20},{20... | collective-permute-start | bytes 4423688 | tf_op jit(solution)/shard_map/ppermute | solution.py:43
  59.3 19.7 %collective-permute-start.16 = (bf16[384,1920]{1,0:T(8,128)(2,1)}, bf16[384,1920]{1,0:T(8,128)(2,1)}, u32[]{:S(2)}, u32[]{:S(2)}) collective-permute-start(bf16[384,1920]{1,0:T(8,128)(2,1)} %constant_dynamic-update-slice_fusion.7.refs_3_.refs_0_.um), channel_id=1, source_target_pairs={{0,2},{1,3},{2,0},{3,1},{4,6},{5,7},{6,4},{7,5},{8,10},{9,11},{10,... | collective-permute-start | bytes 4423688 | tf_op jit(solution)/shard_map/ppermute | solution.py:50
  59.8 11.2 %collective-permute-start.11 = (bf16[384,384]{1,0:T(8,128)(2,1)S(1)}, bf16[384,384]{1,0:T(8,128)(2,1)S(1)}, u32[]{:S(2)}, u32[]{:S(2)}) collective-permute-start(bf16[384,384]{1,0:T(8,128)(2,1)S(1)} %constant_dynamic-update-slice_fusion.5), channel_id=1, source_target_pairs={{0,4},{1,5},{2,6},{3,7},{4,0},{5,1},{6,2},{7,3},{8,12},{9,13},{10,... | collective-permute-start | bytes 884744 | tf_op jit(solution)/shard_map/ppermute | solution.py:50
  87.3 14.8 %collective-permute-start.18 = (bf16[1536,384]{1,0:T(8,128)(2,1)S(1)}, bf16[1536,384]{1,0:T(8,128)(2,1)S(1)}, u32[]{:S(2)}, u32[]{:S(2)}) collective-permute-start(bf16[1536,384]{1,0:T(8,128)(2,1)S(1)} %constant_dynamic-update-slice_fusion.11.refs_0_), channel_id=1, source_target_pairs={{0,16},{16,0},{1,17},{17,1},{2,18},{18,2},{3,19},{19,3},{4,20},{20... | collective-permute-start | bytes 3538952 | tf_op jit(solution)/shard_map/ppermute | solution.py:43
  87.4 16.3 %collective-permute-start.19 = (bf16[1536,384]{1,0:T(8,128)(2,1)S(1)}, bf16[1536,384]{1,0:T(8,128)(2,1)S(1)}, u32[]{:S(2)}, u32[]{:S(2)}) collective-permute-start(bf16[1536,384]{1,0:T(8,128)(2,1)S(1)} %constant_dynamic-update-slice_fusion.11.refs_0_), channel_id=1, source_target_pairs={{0,2},{1,3},{2,0},{3,1},{4,6},{5,7},{6,4},{7,5},{8,10},{9,11},{10,... | collective-permute-start | bytes 3538952 | tf_op jit(solution)/shard_map/ppermute | solution.py:50
  106.5 10.9 %collective-permute-start.21 = (bf16[3072,512]{1,0:T(8,128)(2,1)S(1)}, bf16[3072,512]{1,0:T(8,128)(2,1)S(1)}, u32[]{:S(2)}, u32[]{:S(2)}) collective-permute-start(bf16[3072,512]{1,0:T(8,128)(2,1)S(1)} %get-tuple-element.173.lm), channel_id=1, source_target_pairs={{0,16},{16,0},{1,17},{17,1},{2,18},{18,2},{3,19},{19,3},{4,20},{20... | collective-permute-start | bytes 9437192 | tf_op jit(solution)/shard_map/ppermute | solution.py:43
  129.1 16.2 %collective-permute-start.25 = (bf16[1536,384]{1,0:T(8,128)(2,1)S(1)}, bf16[1536,384]{1,0:T(8,128)(2,1)S(1)}, u32[]{:S(2)}, u32[]{:S(2)}) collective-permute-start(bf16[1536,384]{1,0:T(8,128)(2,1)S(1)} %get-tuple-element.176), channel_id=1, source_target_pairs={{0,2},{1,3},{2,0},{3,1},{4,6},{5,7},{6,4},{7,5},{8,10},{9,11},{10,... | collective-permute-start | bytes 3538952 | tf_op jit(solution)/shard_map/ppermute | solution.py:50
  139.7 24.6 %collective-permute-start.27 = (bf16[384,1536]{1,0:T(8,128)(2,1)S(1)}, bf16[384,1536]{1,0:T(8,128)(2,1)S(1)}, u32[]{:S(2)}, u32[]{:S(2)}) collective-permute-start(bf16[384,1536]{1,0:T(8,128)(2,1)S(1)} %get-tuple-element.184), channel_id=1, source_target_pairs={{0,2},{1,3},{2,0},{3,1},{4,6},{5,7},{6,4},{7,5},{8,10},{9,11},{10,... | collective-permute-start | bytes 3538952 | tf_op jit(solution)/shard_map/ppermute | solution.py:50
  141.3 24.7 %collective-permute-start.28 = (bf16[768,512]{1,0:T(8,128)(2,1)S(1)}, bf16[768,512]{1,0:T(8,128)(2,1)S(1)}, u32[]{:S(2)}, u32[]{:S(2)}) collective-permute-start(bf16[768,512]{1,0:T(8,128)(2,1)S(1)} %copy-done.6), channel_id=1, source_target_pairs={{0,16},{16,0},{1,17},{17,1},{2,18},{18,2},{3,19},{19,3},{4,20},{20... | collective-permute-start | bytes 2359304 | tf_op jit(solution)/shard_map/ppermute | solution.py:43
  141.3 24.9 %collective-permute-start.31 = (bf16[768,512]{1,0:T(8,128)(2,1)S(1)}, bf16[768,512]{1,0:T(8,128)(2,1)S(1)}, u32[]{:S(2)}, u32[]{:S(2)}) collective-permute-start(bf16[768,512]{1,0:T(8,128)(2,1)S(1)} %get-tuple-element.210.refs_6_), channel_id=1, source_target_pairs={{0,16},{16,0},{1,17},{17,1},{2,18},{18,2},{3,19},{19,3},{4,20},{20... | collective-permute-start | bytes 2359304 | tf_op jit(solution)/shard_map/ppermute | solution.py:43
  145.5 18.9 %collective-permute-start.26 = (bf16[768,384]{1,0:T(8,128)(2,1)S(1)}, bf16[768,384]{1,0:T(8,128)(2,1)S(1)}, u32[]{:S(2)}, u32[]{:S(2)}) collective-permute-start(bf16[768,384]{1,0:T(8,128)(2,1)S(1)} %reduce-precision_convert_fusion.1), channel_id=1, source_target_pairs={{0,1},{1,0},{2,3},{3,2},{4,5},{5,4},{6,7},{7,6},{8,9},{9,8},{10,11... | collective-permute-start | bytes 1769480 | tf_op jit(solution)/shard_map/ppermute | solution.py:50
  156.2 11.5 %collective-permute-start.29 = (bf16[3584,128]{1,0:T(8,128)(2,1)S(1)}, bf16[3584,128]{1,0:T(8,128)(2,1)S(1)}, u32[]{:S(2)}, u32[]{:S(2)}) collective-permute-start(bf16[3584,128]{1,0:T(8,128)(2,1)S(1)} %get-tuple-element.208.refs_0_), channel_id=1, source_target_pairs={{0,16},{16,0},{1,17},{17,1},{2,18},{18,2},{3,19},{19,3},{4,20},{20... | collective-permute-start | bytes 2752520 | tf_op jit(solution)/shard_map/ppermute | solution.py:43
  164.4 11.2 %collective-permute-start.35 = (bf16[192,1536]{1,0:T(8,128)(2,1)S(1)}, bf16[192,1536]{1,0:T(8,128)(2,1)S(1)}, u32[]{:S(2)}, u32[]{:S(2)}) collective-permute-start(bf16[192,1536]{1,0:T(8,128)(2,1)S(1)} %reduce-precision_convert_fusion), channel_id=1, source_target_pairs={{0,1},{1,0},{2,3},{3,2},{4,5},{5,4},{6,7},{7,6},{8,9},{9,8},{10,11... | collective-permute-start | bytes 1769480 | tf_op jit(solution)/shard_map/ppermute | solution.py:50
  171.2 14.4 %collective-permute-start.33 = (bf16[384,1152]{1,0:T(8,128)(2,1)S(1)}, bf16[384,1152]{1,0:T(8,128)(2,1)S(1)}, u32[]{:S(2)}, u32[]{:S(2)}) collective-permute-start(bf16[384,1152]{1,0:T(8,128)(2,1)S(1)} %get-tuple-element.214), channel_id=1, source_target_pairs={{0,2},{1,3},{2,0},{3,1},{4,6},{5,7},{6,4},{7,5},{8,10},{9,11},{10,... | collective-permute-start | bytes 2654216 | tf_op jit(solution)/shard_map/ppermute | solution.py:50
  175.8 11.9 %collective-permute-start.36 = (bf16[96,1536]{1,0:T(8,128)(2,1)S(1)}, bf16[96,1536]{1,0:T(8,128)(2,1)S(1)}, u32[]{:S(2)}, u32[]{:S(2)}) collective-permute-start(bf16[96,1536]{1,0:T(8,128)(2,1)S(1)} %reduce-precision_convert_fusion.3), channel_id=1, source_target_pairs={{0,4},{1,5},{2,6},{3,7},{4,0},{5,1},{6,2},{7,3},{8,12},{9,13},{10,... | collective-permute-start | bytes 884744 | tf_op jit(solution)/shard_map/ppermute | solution.py:50
  187.8 11.4 %collective-permute-start.39 = (bf16[192,1152]{1,0:T(8,128)(2,1)S(1)}, bf16[192,1152]{1,0:T(8,128)(2,1)S(1)}, u32[]{:S(2)}, u32[]{:S(2)}) collective-permute-start(bf16[192,1152]{1,0:T(8,128)(2,1)S(1)} %reduce-precision_convert_fusion.2), channel_id=1, source_target_pairs={{0,1},{1,0},{2,3},{3,2},{4,5},{5,4},{6,7},{7,6},{8,9},{9,8},{10,11... | collective-permute-start | bytes 1327112 | tf_op jit(solution)/shard_map/ppermute | solution.py:50
  188.2 10.9 %collective-permute-start.48 = (bf16[48,1536]{1,0:T(8,128)(2,1)S(1)}, bf16[48,1536]{1,0:T(8,128)(2,1)S(1)}, u32[]{:S(2)}, u32[]{:S(2)}) collective-permute-start(bf16[48,1536]{1,0:T(8,128)(2,1)S(1)} %reduce-precision_convert_fusion.9), channel_id=1, source_target_pairs={{0,8},{1,9},{2,10},{3,11},{4,12},{5,13},{6,14},{7,15},{8,0},{9,1},... | collective-permute-start | bytes 442376 | tf_op jit(solution)/shard_map/ppermute | solution.py:50
  (44 other events, 295.2 us)

commit v3 on v2

--- a/solution.py
+++ b/solution.py
@@ -11,8 +11,8 @@
 LANES = 128
 VECTORS = 16
 VMEM_BYTES = 24 << 20
-FLOPS = 300_000_000
-BYTES = 900_000
+FLOPS = 250_000_000
+BYTES = 750_000
 
 masked_score = -1e30
 norm_eps = 1e-05
@@ -595,7 +595,7 @@
     return pl.pallas_call(
         body,
         name="attend_back",
-        cost_estimate=cost(5),
+        cost_estimate=cost(2),
         out_shape=[shape(sent, LANES, bf16), shape(kept, LANES, bf16)],
         grid_spec=pltpu.PrefetchScalarGridSpec(
             num_scalar_prefetch=1,
@@ -1170,10 +1170,13 @@
     down_sent = half_columns(links, down_weight)
 
     qkv_held = joined(links.cross(qkv_sent))
-    up_held = links.cross(after(up_sent, qkv_held))
+    up_steps = []
+    up_held = links.cross_slowly(
+        after(up_sent, qkv_held), lambda more: (up_steps.append(more), more)[1]
+    )
     down_sent = after(down_sent, up_held)
     qkv_held = links.first(qkv_held)
-    qkv = links.second(after(qkv_held, up_held[1]), *up_held)
+    qkv = links.second(after(qkv_held, *up_steps), *up_held)
     up_held = after(joined(up_held), qkv[0][1])
     query, kv, vectors, up_bias_row, rows_t = project(
         links, table, after(rows, up_held), qkv, qkv_piece, vector_piece, scale, base, folds

time: 223 us -> 223 us (level)
  starting transfers between devices: 35.3 us -> 33 us
    ppermute x30 -> x29, starting transfers between devices: 32.4 us -> 30.1 us  [hop(): return lax.ppermute(value, ('ctx', 'dp'), pairs)]
    ppermute x30 -> x29, waiting for transfers between devices: 61 us -> 62.3 us  [hop(): return lax.ppermute(value, ('ctx', 'dp'), pairs)]
  transfers between devices with their start and end apart: 51 -> 50, of which waited for: 28 -> 27; matrix products, arithmetic and copies ran while one was open for 3% -> 4% of each run, Pallas kernels for 40% -> 40%
where the time goes in v3:
time: 223 us; the launch traced here: 222 us
  Pallas kernels  101 us (45%)
  waiting for transfers between devices  72.4 us (32%)
  starting transfers between devices  33 us (15%)
  local copies, waits for them, and re-layouts  10.2 us (5%)
  other arithmetic  3.64 us (2%)
    pallas_call x13, Pallas kernels, call(): pl.pallas_call(body, name=name, out_shape=outs, in_specs=in_specs, out_sp...  63 us
    ppermute x29, waiting for transfers between devices, hop(): return lax.ppermute(value, ('ctx', 'dp'), pairs)  62.3 us
    ppermute x29, starting transfers between devices, hop(): return lax.ppermute(value, ('ctx', 'dp'), pairs)  30.1 us
    pallas_call x3, Pallas kernels, attend_back(): pl.pallas_call(body, name='attend_back', cost_estimate=cost(2), out_shape...  19 us
    pallas_call x3, Pallas kernels, attend(): pl.pallas_call(body, name='attend', cost_estimate=cost(8), out_shape=[in_...  18.7 us
    ppermute x21, waiting for transfers between devices, swap(): return lax.ppermute(value, 'ctx', [(i, i ^ 1) for i in range(self.ctx)])  10.1 us
  transfers between devices with their start and end apart: 50, of which 27 were waited for; matrix products, arithmetic and copies ran while one was open for 4% of the time, Pallas kernels for 40%

profile of v3, /device:TPU:0, one launch (start us, length us, event | category | flops | bytes accessed | tf_op | source)
XLA Modules:
  0.0 222.0 jit_solution(14652911463183275978)
XLA Ops:
  3.4 5.1 %collective-permute-start.2 = (bf16[48,1280]{1,0:T(8,128)(2,1)S(1)}, bf16[48,1280]{1,0:T(8,128)(2,1)S(1)}, u32[]{:S(2)}, u32[]{:S(2)}) collective-permute-start(bf16[48,1280]{1,0:T(8,128)(2,1)S(1)} %get-tuple-element.261), channel_id=1, source_target_pairs={{0,12},{1,13},{2,14},{3,15},{4,8},{5,9},{6,10},{7,11},{8,4},{9,5},... | collective-permute-start | bytes 368648 | tf_op jit(solution)/shard_map/ppermute | solution.py:50
  21.5 6.4 %collective-permute-done.5 = bf16[192,1280]{1,0:T(8,128)(2,1)S(1)} collective-permute-done((bf16[192,1280]{1,0:T(8,128)(2,1)S(1)}, bf16[192,1280]{1,0:T(8,128)(2,1)S(1)}, u32[]{:S(2)}, u32[]{:S(2)}) %collective-permute-start.5) | collective-permute-done | bytes 491552 | tf_op jit(solution)/shard_map/ppermute | solution.py:50
  31.5 11.2 %collective-permute-done.4 = bf16[96,1920]{1,0:T(8,128)(2,1)S(1)} collective-permute-done((bf16[96,1920]{1,0:T(8,128)(2,1)S(1)}, bf16[96,1920]{1,0:T(8,128)(2,1)S(1)}, u32[]{:S(2)}, u32[]{:S(2)}) %collective-permute-start.4) | collective-permute-done | bytes 368672 | tf_op jit(solution)/shard_map/ppermute | solution.py:50
  48.5 4.9 %qkv.1 = (bf16[512,768]{1,0:T(8,128)(2,1)S(1)}, bf16[512,1536]{1,0:T(8,128)(2,1)S(1)}, f32[16,768]{1,0:T(8,128)S(1)}, f32[1,3072]{1,0:T(1,128)S(1)}, bf16[768,512]{1,0:T(8,128)(2,1)}) custom-call(s32[67]{0:T(128)S(1)} %concatenate.46.scalar, bf16[512,768]{1,0:T(8,128)(2,1)S(1)} %bitcast.33, bf16[384,1280]{1,0:T(8,128)(2,1)} %copy-done.14, ...), custom_call_target="tpu_custom_call" | custom-call | flops 1250000000 | bytes 3750000 | tf_op jit(solution)/shard_map/qkv/pallas_call | solution.py:228
  53.3 3.4 %collective-permute-done.11 = bf16[192,1920]{1,0:T(8,128)(2,1)} collective-permute-done((bf16[192,1920]{1,0:T(8,128)(2,1)S(1)}, bf16[192,1920]{1,0:T(8,128)(2,1)}, u32[]{:S(2)}, u32[]{:S(2)}) %collective-permute-start.11) | collective-permute-done | bytes 737312 | tf_op jit(solution)/shard_map/ppermute | solution.py:50
  60.0 3.7 %collective-permute-done.12.refs_2_.refs_3_ = bf16[512,1536]{1,0:T(8,128)(2,1)S(1)} collective-permute-done((bf16[512,1536]{1,0:T(8,128)(2,1)S(1)}, bf16[512,1536]{1,0:T(8,128)(2,1)S(1)}, u32[]{:S(2)}, u32[]{:S(2)}) %collective-permute-start.12) | collective-permute-done | bytes 1572896 | tf_op jit(solution)/shard_map/ppermute | solution.py:43
  64.8 6.2 %attend.3 = (f32[256,512]{1,0:T(8,128)}, bf16[512,256]{1,0:T(8,128)(2,1)S(1)}, bf16[2,1024,1024]{2,1,0:T(8,128)(2,1)}, f32[2,1,1024]{2,1,0:T(1,128)}) custom-call(s32[3]{0:T(128)S(1)} %pad_add_fusion.scalar, bf16[512,768]{1,0:T(8,128)(2,1)S(1)} %copy-done.3, bf16[512,1536]{1,0:T(8,128)(2,1)S(1)} %get-tuple-element.148.refs_0_.refs_1_, ...), custom_call_target="tpu_custom_call" | custom-call | flops 2000000000 | bytes 6000000 | tf_op jit(solution)/shard_map/attend/pallas_call | solution.py:479
  71.1 6.2 %attend.4 = (f32[256,512]{1,0:T(8,128)}, bf16[512,256]{1,0:T(8,128)(2,1)S(1)}, bf16[2,1024,1024]{2,1,0:T(8,128)(2,1)}, f32[2,1,1024]{2,1,0:T(1,128)}) custom-call(s32[3]{0:T(128)S(1)} %pad_add_fusion.scalar, bf16[512,768]{1,0:T(8,128)(2,1)S(1)} %copy-done.3, bf16[512,1536]{1,0:T(8,128)(2,1)S(1)} %get-tuple-element.148.refs_0_.refs_1_, ...), custom_call_target="tpu_custom_call" | custom-call | flops 2000000000 | bytes 6000000 | tf_op jit(solution)/shard_map/attend/pallas_call | solution.py:479
  79.0 6.3 %attend.5 = (f32[256,512]{1,0:T(8,128)}, bf16[512,256]{1,0:T(8,128)(2,1)S(1)}, bf16[2,1024,1024]{2,1,0:T(8,128)(2,1)}, f32[2,1,1024]{2,1,0:T(1,128)}) custom-call(s32[3]{0:T(128)S(1)} %pad_add_fusion.scalar, bf16[512,768]{1,0:T(8,128)(2,1)S(1)} %copy-done.3, bf16[512,1536]{1,0:T(8,128)(2,1)S(1)} %get-tuple-element.148.refs_0_.refs_1_, ...), custom_call_target="tpu_custom_call" | custom-call | flops 2000000000 | bytes 6000000 | tf_op jit(solution)/shard_map/attend/pallas_call | solution.py:479
  89.1 4.4 %after_attention.1 = (f32[512,768]{1,0:T(8,128)S(1)}, bf16[512,768]{1,0:T(8,128)(2,1)S(1)}, bf16[768,512]{1,0:T(8,128)(2,1)S(1)}, bf16[768,512]{1,0:T(8,128)(2,1...) custom-call(s32[67]{0:T(128)S(1)} %concatenate.46.scalar, ...), custom_call_target="tpu_custom_call" | custom-call | flops 875000000 | bytes 2625000 | tf_op jit(solution)/shard_map/after_attention/pallas_call | solution.py:228
  93.5 8.6 %feed_up.1 = (bf16[512,3072]{1,0:T(8,128)(2,1)S(1)}, bf16[3072,512]{1,0:T(8,128)(2,1)S(1)}, bf16[512,3072]{1,0:T(8,128)(2,1)S(1)}) custom-call(s32[67]{0:T(128)S(1)} %concatenate.46.scalar, bf16[512,768]{1,0:T(8,128)(2,1)S(1)} %get-tuple-element.162.low_ref, f32[1,3072]{1,0:T(1,128)S(1)} %get-tuple-element.163.bias_ref, ...), custom_call_target="tpu_custom_call" | custom-call | flops 2000000000 | bytes 6000000 | tf_op jit(solution)/shard_map/feed_up/pallas_call | solution.py:228
  107.6 8.1 %feed_down.1 = (bf16[512,768]{1,0:T(8,128)(2,1)}, f32[512,768]{1,0:T(8,128)S(1)}, bf16[512,768]{1,0:T(8,128)(2,1)S(1)}, bf16[512,384]{1,0:T(8,128)(2,1)S(1)}, bf...) custom-call(s32[67]{0:T(128)S(1)} %concatenate.46.scalar, bf16[512,3072]{1,0:T(8,128)(2,1)S(1)} %get-tuple-element.164.act_ref, ...), custom_call_target="tpu_custom_call" | custom-call | flops 1500000000 | bytes 4500000 | tf_op jit(solution)/shard_map/feed_down/pallas_call | solution.py:228
  117.5 4.8 %down_gradient.1 = (bf16[768,384]{1,0:T(8,128)(2,1)S(1)}, bf16[768,384]{1,0:T(8,128)(2,1)S(1)}, bf16[1536,384]{1,0:T(8,128)(2,1)S(1)}) custom-call(s32[67]{0:T(128)S(1)} %concatenate.46.scalar, bf16[3072,512]{1,0:T(8,128)(2,1)S(1)} %get-tuple-element.173.lm, bf16[3072,512]{1,0:T(8,128)(2,1)S(1)} %collective-permute-done.20.lt, ...), custom_call_target="tpu_custom_call" | custom-call | flops 1250000000 | bytes 3750000 | tf_op jit(solution)/shard_map/down_gradient/pallas_call | solution.py:228
  122.3 6.2 %feed_back.2 = (f32[512,768]{1,0:T(8,128)S(1)}, bf16[512,1536]{1,0:T(8,128)(2,1)S(1)}, f32[1,1536]{1,0:T(1,128)S(1)}) custom-call(s32[67]{0:T(128)S(1)} %concatenate.46.scalar, bf16[512,3072]{1,0:T(8,128)(2,1)S(1)} %get-tuple-element.170.slope_ref, f32[512,768]{1,0:T(8,128)S(1)} %get-tuple-element.177.so_far_ref, ...), custom_call_target="tpu_custom_call" | custom-call | flops 2500000 | bytes 7500 | tf_op jit(solution)/shard_map/feed_back/pallas_call | solution.py:228
  129.6 6.2 %feed_back.3 = (f32[512,768]{1,0:T(8,128)S(1)}, bf16[512,1536]{1,0:T(8,128)(2,1)S(1)}, f32[1,1536]{1,0:T(1,128)S(1)}) custom-call(s32[67]{0:T(128)S(1)} %concatenate.46.scalar, bf16[512,3072]{1,0:T(8,128)(2,1)S(1)} %get-tuple-element.170.slope_ref, f32[512,768]{1,0:T(8,128)S(1)} %get-tuple-element.179.so_far_ref, ...), custom_call_target="tpu_custom_call" | custom-call | flops 2500000 | bytes 7500 | tf_op jit(solution)/shard_map/feed_back/pallas_call | solution.py:228
  135.8 3.8 %up_gradient.1 = (bf16[192,1536]{1,0:T(8,128)(2,1)S(1)}, bf16[192,1536]{1,0:T(8,128)(2,1)S(1)}, bf16[384,1536]{1,0:T(8,128)(2,1)S(1)}) custom-call(s32[67]{0:T(128)S(1)} %concatenate.46.scalar, bf16[768,512]{1,0:T(8,128)(2,1)S(1)} %get-tuple-element.181.lm, bf16[768,512]{1,0:T(8,128)(2,1)S(1)} %collective-permute-done.22.lt, ...), custom_call_target="tpu_custom_call" | custom-call | flops 1250000000 | bytes 3750000 | tf_op jit(solution)/shard_map/up_gradient/pallas_call | solution.py:228
  141.8 3.5 %collective-permute-done.24 = bf16[1536,384]{1,0:T(8,128)(2,1)S(1)} collective-permute-done((bf16[1536,384]{1,0:T(8,128)(2,1)S(1)}, bf16[1536,384]{1,0:T(8,128)(2,1)S(1)}, u32[]{:S(2)}, u32[]{:S(2)}) %collective-permute-start.24) | collective-permute-done | bytes 1179680 | tf_op jit(solution)/shard_map/ppermute | solution.py:50
  149.9 6.3 %attend_back.3 = (bf16[3584,128]{1,0:T(8,128)(2,1)S(1)}, bf16[1536,128]{1,0:T(8,128)(2,1)S(1)}) custom-call(s32[1]{0:T(128)} %bitcast._, bf16[512,768]{1,0:T(8,128)(2,1)S(1)} %copy-done.4, bf16[512,768]{1,0:T(8,128)(2,1)S(1)} %get-tuple-element.193.gm_ref, f32[256,512]{1,0:T(8,128)} %get-tuple-element.195.mt_ref, ...), custom_call_target="tpu_custom_call" | custom-call | flops 500000000 | bytes 1500000 | tf_op jit(solution)/shard_map/attend_back/pallas_call | solution.py:595
  156.3 6.5 %attend_back.4 = (bf16[3584,128]{1,0:T(8,128)(2,1)S(1)}, bf16[1536,128]{1,0:T(8,128)(2,1)S(1)}) custom-call(s32[1]{0:T(128)} %bitcast._, bf16[512,768]{1,0:T(8,128)(2,1)S(1)} %copy-done.4, bf16[512,768]{1,0:T(8,128)(2,1)S(1)} %get-tuple-element.193.gm_ref, f32[256,512]{1,0:T(8,128)} %get-tuple-element.200.mt_ref, ...), custom_call_target="tpu_custom_call" | custom-call | flops 500000000 | bytes 1500000 | tf_op jit(solution)/shard_map/attend_back/pallas_call | solution.py:595
  167.7 3.5 %early_gradient.1 = (bf16[192,1152]{1,0:T(8,128)(2,1)S(1)}, bf16[192,1152]{1,0:T(8,128)(2,1)S(1)}, bf16[384,1152]{1,0:T(8,128)(2,1)S(1)}, f32[2,384]{1,0:T(2,128)S(1)}) custom-call(s32[67]{0:T(128)S(1)} %concatenate.46.scalar, bf16[768,512]{1,0:T(8,128)(2,1)S(1)} %copy-done.8, bf16[768,512]{1,0:T(8,128)(2,1)S(1)} %collective-permute-done.27.xt, ...), custom_call_target="tpu_custom_call" | custom-call | flops 1250000000 | bytes 3750000 | tf_op jit(solution)/shard_map/early_gradient/pallas_call | solution.py:228
  171.8 3.8 %collective-permute-done.33 = bf16[384,384]{1,0:T(8,128)(2,1)S(1)} collective-permute-done((bf16[384,384]{1,0:T(8,128)(2,1)S(1)}, bf16[384,384]{1,0:T(8,128)(2,1)S(1)}, u32[]{:S(2)}, u32[]{:S(2)}) %collective-permute-start.33) | collective-permute-done | bytes 294944 | tf_op jit(solution)/shard_map/ppermute | solution.py:50
  178.3 6.2 %attend_back.5 = (bf16[3584,128]{1,0:T(8,128)(2,1)S(1)}, bf16[1536,128]{1,0:T(8,128)(2,1)S(1)}) custom-call(s32[1]{0:T(128)} %bitcast._, bf16[512,768]{1,0:T(8,128)(2,1)S(1)} %copy-done.4, bf16[512,768]{1,0:T(8,128)(2,1)S(1)} %get-tuple-element.193.gm_ref, f32[256,512]{1,0:T(8,128)} %get-tuple-element.219.mt_ref, ...), custom_call_target="tpu_custom_call" | custom-call | flops 500000000 | bytes 1500000 | tf_op jit(solution)/shard_map/attend_back/pallas_call | solution.py:595
  193.2 5.8 %input_gradient.1 = f32[512,768]{1,0:T(8,128)} custom-call(s32[67]{0:T(128)S(1)} %concatenate.46.scalar, f32[512,768]{1,0:T(8,128)S(1)} %get-tuple-element.237.resid_ref, bf16[3584,128]{1,0:T(8,128)(2,1)S(1)} %get-tuple-element.208.refs_0_, bf16[1536,128]{1,0:T(8,128)(2,1)S(1)} %get-tuple-element.198.refs_1_, ...), custom_call_target="tpu_custom_call" | custom-call | flops 5000000000 | bytes 15000000 | tf_op jit(solution)/shard_map/input_gradient/pallas_call | solution.py:228
  202.9 4.6 %collective-permute-done.43 = bf16[192,512]{1,0:T(8,128)(2,1)S(1)} collective-permute-done((bf16[192,512]{1,0:T(8,128)(2,1)S(1)}, bf16[192,512]{1,0:T(8,128)(2,1)S(1)}, u32[]{:S(2)}, u32[]{:S(2)}) %collective-permute-start.43) | collective-permute-done | bytes 196640 | tf_op jit(solution)/shard_map/ppermute | solution.py:50
  (179 shorter events, 84.2 us)
Async XLA Ops:
  8.6 10.4 %collective-permute-start = (bf16[48,1280]{1,0:T(8,128)(2,1)S(1)}, bf16[48,1280]{1,0:T(8,128)(2,1)S(1)}, u32[]{:S(2)}, u32[]{:S(2)}) collective-permute-start(bf16[48,1280]{1,0:T(8,128)(2,1)S(1)} %get-tuple-element.261), channel_id=1, source_target_pairs={{0,8},{1,9},{2,10},{3,11},{4,12},{5,13},{6,14},{7,15},{8,0},{9,1},... | collective-permute-start | bytes 368648 | tf_op jit(solution)/shard_map/ppermute | solution.py:50
  20.5 10.3 %collective-permute-start.3 = (bf16[48,1920]{1,0:T(8,128)(2,1)S(1)}, bf16[48,1920]{1,0:T(8,128)(2,1)S(1)}, u32[]{:S(2)}, u32[]{:S(2)}) collective-permute-start(bf16[48,1920]{1,0:T(8,128)(2,1)S(1)} %pad_maximum_fusion.2), channel_id=1, source_target_pairs={{0,8},{1,9},{2,10},{3,11},{4,12},{5,13},{6,14},{7,15},{8,0},{9,1},... | collective-permute-start | bytes 552968 | tf_op jit(solution)/shard_map/ppermute | solution.py:50
  30.8 11.9 %collective-permute-start.6 = (bf16[384,1280]{1,0:T(8,128)(2,1)S(1)}, bf16[384,1280]{1,0:T(8,128)(2,1)S(1)}, u32[]{:S(2)}, u32[]{:S(2)}) collective-permute-start(bf16[384,1280]{1,0:T(8,128)(2,1)S(1)} %constant_dynamic-update-slice_fusion.2.refs_0_.refs_9_), channel_id=1, source_target_pairs={{0,16},{16,0},{1,17},{17,1},{2,18},{18,2},{3,19},{19,3},{4,20},{20... | collective-permute-start | bytes 2949128 | tf_op jit(solution)/shard_map/ppermute | solution.py:43
  30.8 14.2 %collective-permute-start.7 = (bf16[384,1280]{1,0:T(8,128)(2,1)S(1)}, bf16[384,1280]{1,0:T(8,128)(2,1)}, u32[]{:S(2)}, u32[]{:S(2)}) collective-permute-start(bf16[384,1280]{1,0:T(8,128)(2,1)S(1)} %constant_dynamic-update-slice_fusion.2.refs_0_.refs_9_), channel_id=1, source_target_pairs={{0,2},{1,3},{2,0},{3,1},{4,6},{5,7},{6,4},{7,5},{8,10},{9,11},{10,... | collective-permute-start | bytes 2949128 | tf_op jit(solution)/shard_map/ppermute | solution.py:50
  31.4 11.3 %collective-permute-start.4 = (bf16[96,1920]{1,0:T(8,128)(2,1)S(1)}, bf16[96,1920]{1,0:T(8,128)(2,1)S(1)}, u32[]{:S(2)}, u32[]{:S(2)}) collective-permute-start(bf16[96,1920]{1,0:T(8,128)(2,1)S(1)} %constant_dynamic-update-slice_fusion), channel_id=1, source_target_pairs={{0,4},{1,5},{2,6},{3,7},{4,0},{5,1},{6,2},{7,3},{8,12},{9,13},{10,... | collective-permute-start | bytes 1105928 | tf_op jit(solution)/shard_map/ppermute | solution.py:50
  45.1 11.6 %collective-permute-start.11 = (bf16[192,1920]{1,0:T(8,128)(2,1)S(1)}, bf16[192,1920]{1,0:T(8,128)(2,1)}, u32[]{:S(2)}, u32[]{:S(2)}) collective-permute-start(bf16[192,1920]{1,0:T(8,128)(2,1)S(1)} %pad_maximum_fusion), channel_id=1, source_target_pairs={{0,1},{1,0},{2,3},{3,2},{4,5},{5,4},{6,7},{7,6},{8,9},{9,8},{10,11... | collective-permute-start | bytes 2211848 | tf_op jit(solution)/shard_map/ppermute | solution.py:50
  47.5 11.3 %collective-permute-start.8 = (bf16[192,384]{1,0:T(8,128)(2,1)S(1)}, bf16[192,384]{1,0:T(8,128)(2,1)S(1)}, u32[]{:S(2)}, u32[]{:S(2)}) collective-permute-start(bf16[192,384]{1,0:T(8,128)(2,1)S(1)} %constant_dynamic-slice_fusion.3), channel_id=1, source_target_pairs={{0,8},{1,9},{2,10},{3,11},{4,12},{5,13},{6,14},{7,15},{8,0},{9,1},... | collective-permute-start | bytes 442376 | tf_op jit(solution)/shard_map/ppermute | solution.py:50
  58.8 20.1 %collective-permute-start.14 = (bf16[384,1920]{1,0:T(8,128)(2,1)}, bf16[384,1920]{1,0:T(8,128)(2,1)}, u32[]{:S(2)}, u32[]{:S(2)}) collective-permute-start(bf16[384,1920]{1,0:T(8,128)(2,1)} %constant_dynamic-update-slice_fusion.9.refs_3_.refs_0_.um), channel_id=1, source_target_pairs={{0,16},{16,0},{1,17},{17,1},{2,18},{18,2},{3,19},{19,3},{4,20},{20... | collective-permute-start | bytes 4423688 | tf_op jit(solution)/shard_map/ppermute | solution.py:43
  59.3 19.7 %collective-permute-start.15 = (bf16[384,1920]{1,0:T(8,128)(2,1)}, bf16[384,1920]{1,0:T(8,128)(2,1)}, u32[]{:S(2)}, u32[]{:S(2)}) collective-permute-start(bf16[384,1920]{1,0:T(8,128)(2,1)} %constant_dynamic-update-slice_fusion.9.refs_3_.refs_0_.um), channel_id=1, source_target_pairs={{0,2},{1,3},{2,0},{3,1},{4,6},{5,7},{6,4},{7,5},{8,10},{9,11},{10,... | collective-permute-start | bytes 4423688 | tf_op jit(solution)/shard_map/ppermute | solution.py:50
  59.8 11.2 %collective-permute-start.10 = (bf16[384,384]{1,0:T(8,128)(2,1)S(1)}, bf16[384,384]{1,0:T(8,128)(2,1)S(1)}, u32[]{:S(2)}, u32[]{:S(2)}) collective-permute-start(bf16[384,384]{1,0:T(8,128)(2,1)S(1)} %constant_dynamic-update-slice_fusion.7), channel_id=1, source_target_pairs={{0,4},{1,5},{2,6},{3,7},{4,0},{5,1},{6,2},{7,3},{8,12},{9,13},{10,... | collective-permute-start | bytes 884744 | tf_op jit(solution)/shard_map/ppermute | solution.py:50
  87.3 14.8 %collective-permute-start.17 = (bf16[1536,384]{1,0:T(8,128)(2,1)S(1)}, bf16[1536,384]{1,0:T(8,128)(2,1)S(1)}, u32[]{:S(2)}, u32[]{:S(2)}) collective-permute-start(bf16[1536,384]{1,0:T(8,128)(2,1)S(1)} %constant_dynamic-update-slice_fusion.13.refs_0_), channel_id=1, source_target_pairs={{0,16},{16,0},{1,17},{17,1},{2,18},{18,2},{3,19},{19,3},{4,20},{20... | collective-permute-start | bytes 3538952 | tf_op jit(solution)/shard_map/ppermute | solution.py:43
  87.4 16.3 %collective-permute-start.18 = (bf16[1536,384]{1,0:T(8,128)(2,1)S(1)}, bf16[1536,384]{1,0:T(8,128)(2,1)S(1)}, u32[]{:S(2)}, u32[]{:S(2)}) collective-permute-start(bf16[1536,384]{1,0:T(8,128)(2,1)S(1)} %constant_dynamic-update-slice_fusion.13.refs_0_), channel_id=1, source_target_pairs={{0,2},{1,3},{2,0},{3,1},{4,6},{5,7},{6,4},{7,5},{8,10},{9,11},{10,... | collective-permute-start | bytes 3538952 | tf_op jit(solution)/shard_map/ppermute | solution.py:50
  106.5 11.0 %collective-permute-start.20 = (bf16[3072,512]{1,0:T(8,128)(2,1)S(1)}, bf16[3072,512]{1,0:T(8,128)(2,1)S(1)}, u32[]{:S(2)}, u32[]{:S(2)}) collective-permute-start(bf16[3072,512]{1,0:T(8,128)(2,1)S(1)} %get-tuple-element.173.lm), channel_id=1, source_target_pairs={{0,16},{16,0},{1,17},{17,1},{2,18},{18,2},{3,19},{19,3},{4,20},{20... | collective-permute-start | bytes 9437192 | tf_op jit(solution)/shard_map/ppermute | solution.py:43
  129.1 16.2 %collective-permute-start.24 = (bf16[1536,384]{1,0:T(8,128)(2,1)S(1)}, bf16[1536,384]{1,0:T(8,128)(2,1)S(1)}, u32[]{:S(2)}, u32[]{:S(2)}) collective-permute-start(bf16[1536,384]{1,0:T(8,128)(2,1)S(1)} %get-tuple-element.176), channel_id=1, source_target_pairs={{0,2},{1,3},{2,0},{3,1},{4,6},{5,7},{6,4},{7,5},{8,10},{9,11},{10,... | collective-permute-start | bytes 3538952 | tf_op jit(solution)/shard_map/ppermute | solution.py:50
  139.7 24.6 %collective-permute-start.26 = (bf16[384,1536]{1,0:T(8,128)(2,1)S(1)}, bf16[384,1536]{1,0:T(8,128)(2,1)S(1)}, u32[]{:S(2)}, u32[]{:S(2)}) collective-permute-start(bf16[384,1536]{1,0:T(8,128)(2,1)S(1)} %get-tuple-element.184), channel_id=1, source_target_pairs={{0,2},{1,3},{2,0},{3,1},{4,6},{5,7},{6,4},{7,5},{8,10},{9,11},{10,... | collective-permute-start | bytes 3538952 | tf_op jit(solution)/shard_map/ppermute | solution.py:50
  141.3 24.7 %collective-permute-start.27 = (bf16[768,512]{1,0:T(8,128)(2,1)S(1)}, bf16[768,512]{1,0:T(8,128)(2,1)S(1)}, u32[]{:S(2)}, u32[]{:S(2)}) collective-permute-start(bf16[768,512]{1,0:T(8,128)(2,1)S(1)} %copy-done.8), channel_id=1, source_target_pairs={{0,16},{16,0},{1,17},{17,1},{2,18},{18,2},{3,19},{19,3},{4,20},{20... | collective-permute-start | bytes 2359304 | tf_op jit(solution)/shard_map/ppermute | solution.py:43
  141.3 24.9 %collective-permute-start.30 = (bf16[768,512]{1,0:T(8,128)(2,1)S(1)}, bf16[768,512]{1,0:T(8,128)(2,1)S(1)}, u32[]{:S(2)}, u32[]{:S(2)}) collective-permute-start(bf16[768,512]{1,0:T(8,128)(2,1)S(1)} %get-tuple-element.210.refs_6_), channel_id=1, source_target_pairs={{0,16},{16,0},{1,17},{17,1},{2,18},{18,2},{3,19},{19,3},{4,20},{20... | collective-permute-start | bytes 2359304 | tf_op jit(solution)/shard_map/ppermute | solution.py:43
  145.5 18.9 %collective-permute-start.25 = (bf16[768,384]{1,0:T(8,128)(2,1)S(1)}, bf16[768,384]{1,0:T(8,128)(2,1)S(1)}, u32[]{:S(2)}, u32[]{:S(2)}) collective-permute-start(bf16[768,384]{1,0:T(8,128)(2,1)S(1)} %reduce-precision_convert_fusion.1), channel_id=1, source_target_pairs={{0,1},{1,0},{2,3},{3,2},{4,5},{5,4},{6,7},{7,6},{8,9},{9,8},{10,11... | collective-permute-start | bytes 1769480 | tf_op jit(solution)/shard_map/ppermute | solution.py:50
  156.2 11.5 %collective-permute-start.28 = (bf16[3584,128]{1,0:T(8,128)(2,1)S(1)}, bf16[3584,128]{1,0:T(8,128)(2,1)S(1)}, u32[]{:S(2)}, u32[]{:S(2)}) collective-permute-start(bf16[3584,128]{1,0:T(8,128)(2,1)S(1)} %get-tuple-element.208.refs_0_), channel_id=1, source_target_pairs={{0,16},{16,0},{1,17},{17,1},{2,18},{18,2},{3,19},{19,3},{4,20},{20... | collective-permute-start | bytes 2752520 | tf_op jit(solution)/shard_map/ppermute | solution.py:43
  164.4 11.2 %collective-permute-start.34 = (bf16[192,1536]{1,0:T(8,128)(2,1)S(1)}, bf16[192,1536]{1,0:T(8,128)(2,1)S(1)}, u32[]{:S(2)}, u32[]{:S(2)}) collective-permute-start(bf16[192,1536]{1,0:T(8,128)(2,1)S(1)} %reduce-precision_convert_fusion), channel_id=1, source_target_pairs={{0,1},{1,0},{2,3},{3,2},{4,5},{5,4},{6,7},{7,6},{8,9},{9,8},{10,11... | collective-permute-start | bytes 1769480 | tf_op jit(solution)/shard_map/ppermute | solution.py:50
  171.2 14.4 %collective-permute-start.32 = (bf16[384,1152]{1,0:T(8,128)(2,1)S(1)}, bf16[384,1152]{1,0:T(8,128)(2,1)S(1)}, u32[]{:S(2)}, u32[]{:S(2)}) collective-permute-start(bf16[384,1152]{1,0:T(8,128)(2,1)S(1)} %get-tuple-element.214), channel_id=1, source_target_pairs={{0,2},{1,3},{2,0},{3,1},{4,6},{5,7},{6,4},{7,5},{8,10},{9,11},{10,... | collective-permute-start | bytes 2654216 | tf_op jit(solution)/shard_map/ppermute | solution.py:50
  175.8 11.9 %collective-permute-start.35 = (bf16[96,1536]{1,0:T(8,128)(2,1)S(1)}, bf16[96,1536]{1,0:T(8,128)(2,1)S(1)}, u32[]{:S(2)}, u32[]{:S(2)}) collective-permute-start(bf16[96,1536]{1,0:T(8,128)(2,1)S(1)} %reduce-precision_convert_fusion.3), channel_id=1, source_target_pairs={{0,4},{1,5},{2,6},{3,7},{4,0},{5,1},{6,2},{7,3},{8,12},{9,13},{10,... | collective-permute-start | bytes 884744 | tf_op jit(solution)/shard_map/ppermute | solution.py:50
  187.8 11.3 %collective-permute-start.38 = (bf16[192,1152]{1,0:T(8,128)(2,1)S(1)}, bf16[192,1152]{1,0:T(8,128)(2,1)S(1)}, u32[]{:S(2)}, u32[]{:S(2)}) collective-permute-start(bf16[192,1152]{1,0:T(8,128)(2,1)S(1)} %reduce-precision_convert_fusion.2), channel_id=1, source_target_pairs={{0,1},{1,0},{2,3},{3,2},{4,5},{5,4},{6,7},{7,6},{8,9},{9,8},{10,11... | collective-permute-start | bytes 1327112 | tf_op jit(solution)/shard_map/ppermute | solution.py:50
  188.3 10.9 %collective-permute-start.47 = (bf16[48,1536]{1,0:T(8,128)(2,1)S(1)}, bf16[48,1536]{1,0:T(8,128)(2,1)S(1)}, u32[]{:S(2)}, u32[]{:S(2)}) collective-permute-start(bf16[48,1536]{1,0:T(8,128)(2,1)S(1)} %reduce-precision_convert_fusion.9), channel_id=1, source_target_pairs={{0,8},{1,9},{2,10},{3,11},{4,12},{5,13},{6,14},{7,15},{8,0},{9,1},... | collective-permute-start | bytes 442376 | tf_op jit(solution)/shard_map/ppermute | solution.py:50
  (43 other events, 286.8 us)
